TPU v7x, 1024 devices: a whole 4x4x32 slice. The times are simulated.
1024 devices in a mesh: ctx: 16 (over y, x), exp: 64 (over z, core).
Axes of the slice: x: 4, y: 4, z: 32, core: 2. Of those that a mesh axis runs over, the one named last changes fastest.
Arguments:
- tokens: bfloat16 [8192, 4096], P('exp', 'ctx'), may hold values from -6 to 6
- cotangent: bfloat16 [8192, 4096], P('exp', 'ctx'), may hold values from -6 to 6
- routes: int32 [8192, 8], P('exp'), may hold values from 0 to 127, all different within a row; in each aligned block of 128 rows (0 to 127, 128 to 255, ...) at most 12 rows name the same one
- router_weight: float32 [4096, 128], P('ctx'), may hold values from -0.09375 to 0.09375
- expert_out: bfloat16 [128, 768, 4096], P('exp', None, 'ctx'), may hold values from -6 to 6
Outputs:
- mixed: bfloat16 [8192, 4096], P('exp', 'ctx')
- token_grad: bfloat16 [8192, 4096], P('exp', 'ctx')
- router_grad: float32 [4096, 128], P('ctx')
- slot_grad: bfloat16 [128, 768, 4096], P('exp', None, 'ctx')
Inputs may be any that keep to these rules, and one draw needn't show every extreme that they name: `routes`: each row names 8 different experts; among the rows of one index of exp no expert is named more than 12 times.
All inputs are finite; a program needn't handle non-finite values.
Results may differ from a plain program's by a relative error of at most 0.00105.
Values may be sent and summed in bfloat16 or wider, within the bound.
No kernel may reach another device: no remote copies, remote signals or barrier semaphores. Data moves between devices by JAX's collectives and lax.ppermute only.
A program may use at most 32 MiB of HBM per device.

v0:
```python
import jax
import jax.numpy as jnp
from jax import lax
from jax.sharding import Mesh
from jax.sharding import PartitionSpec as P

CTX = ("ctx_0", "ctx_1")


def from_everyone(array, axis):
    devices = lax.axis_size(axis)
    return lax.all_to_all(
        jnp.broadcast_to(array[None], (devices, *array.shape)), axis, 0, 0, tiled=True
    )


def of_everyone(array, axis):
    return from_everyone(array, axis).sum(axis=0)


def one_axis_at_a_time(array, axes):
    for axis in axes:
        array = lax.psum(array, axis)
    return array


def gathered_total(array, axis):
    return lax.all_gather(array, axis).sum(0)


def body(tokens, cotangent, routes, router_weight, expert_out):
    rows, top = routes.shape
    local = expert_out.shape[0]
    sources = lax.axis_size("exp")
    experts = local * sources
    capacity = expert_out.shape[1] // sources
    width = tokens.shape[1]
    highest = lax.Precision.HIGHEST
    flat = routes.reshape(-1)
    onehot = (flat[:, None] == jnp.arange(experts, dtype=jnp.int32)[None, :]).astype(jnp.int32)
    earlier = jnp.cumsum(onehot, axis=0) - onehot
    position = jnp.sum(earlier * onehot, axis=1)
    target = flat % local * (sources * capacity) + flat // local * capacity + position
    layout = (local, sources, capacity, width)
    buffer_rows = local * sources * capacity
    tokens_wide = tokens.astype(jnp.float32)
    partial_logits = jnp.dot(tokens_wide, router_weight, precision=highest)
    logits = of_everyone(partial_logits, CTX)
    expo = jnp.exp(logits)
    probs = expo / jnp.sum(expo, axis=1, keepdims=True)
    chosen = jnp.take_along_axis(probs, routes, axis=1)
    total = jnp.sum(chosen, axis=1, keepdims=True)
    gates = chosen / total
    returned = lax.all_to_all(
        expert_out.reshape(layout), "exp", split_axis=1, concat_axis=1, tiled=True
    )
    pairs = (
        jnp.take(returned.reshape(buffer_rows, width), target, axis=0)
        .reshape(rows, top, width)
        .astype(jnp.float32)
    )
    mixed = jnp.sum(gates[:, :, None] * pairs, axis=1).astype(jnp.bfloat16)
    partial_dots = jnp.sum(cotangent.astype(jnp.float32)[:, None, :] * pairs, axis=2)
    weighted = (
        gates.reshape(-1)[:, None] * jnp.repeat(cotangent, top, axis=0).astype(jnp.float32)
    ).astype(jnp.bfloat16)
    weighted_send = jnp.zeros((buffer_rows, width), jnp.bfloat16).at[target].set(weighted)
    slot_grad = lax.all_to_all(
        weighted_send.reshape(layout), "exp", split_axis=1, concat_axis=1, tiled=True
    )
    slot_grad = slot_grad.reshape(local, sources * capacity, width)
    dots = one_axis_at_a_time(partial_dots, CTX)
    dchosen = (dots - jnp.sum(dots * gates, axis=1, keepdims=True)) / total
    match = (routes[:, :, None] == jnp.arange(experts, dtype=jnp.int32)[None, None, :]).astype(
        jnp.float32
    )
    spread = jnp.sum(match * dchosen[:, :, None], axis=1)
    dlogits = probs * (spread - jnp.sum(chosen * dchosen, axis=1, keepdims=True))
    token_grad = jnp.dot(dlogits, router_weight.T, precision=highest).astype(jnp.bfloat16)
    partial_router = jnp.dot(tokens_wide.T, dlogits, precision=highest)
    router_grad = gathered_total(partial_router, "exp")
    return (mixed, token_grad, router_grad, slot_grad)


def solution(mesh):
    split = Mesh(mesh.devices.reshape(4, 4, mesh.shape["exp"]), ("ctx_0", "ctx_1", "exp"))
    in_specs = (P("exp", CTX), P("exp", CTX), P("exp", None), P(CTX, None), P("exp", None, CTX))
    out_specs = (P("exp", CTX), P("exp", CTX), P(CTX, None), P("exp", None, CTX))
    return jax.shard_map(body, mesh=split, in_specs=in_specs, out_specs=out_specs, check_vma=False)
```

profile of v0, /device:TPU:5, one launch (start us, length us, event | category | flops | bytes accessed | tf_op | source)
XLA Modules:
  0.0 368.5 jit_solution(890691755723702869)
XLA Ops:
  7.2 0.9 copy-done
  8.1 1.1 fusion.24
  9.1 1.1 broadcast_in_dim.24
  10.2 6.9 %all-to-all-start = ((f32[16,128,128]{2,1,0:T(8,128)}), f32[16,128,128]{2,1,0:T(8,128)S(1)}, u32[]{:S(2)}, u32[]{:S(2)}) async-start(f32[16,128,128]{2,1,0:T(8,128)} %broadcast_in_dim.24), calls=%async_computation | async-start | bytes 2097152 | tf_op jit(solution)/shard_map/all_to_all | solution.py:12
  17.1 2.8 copy.75
  19.9 6.6 %all-to-all-done = f32[16,128,128]{2,1,0:T(8,128)S(1)} async-done(((f32[16,128,128]{2,1,0:T(8,128)}), f32[16,128,128]{2,1,0:T(8,128)S(1)}, u32[]{:S(2)}, u32[]{:S(2)}) %all-to-all-start) | async-done | bytes 1048608 | tf_op jit(solution)/shard_map/all_to_all | solution.py:12
  26.6 35.2 %all-to-all-start.1 = ((bf16[2,64,12,256]{3,0,2,1:T(2,128)(2,1)}), bf16[2,64,12,256]{3,0,2,1:T(2,128)(2,1)S(1)}, u32[]{:S(2)}, u32[]{:S(2)}) async-start(bf16[2,64,12,256]{3,0,2,1:T(2,128)(2,1)} %bitcast.4), calls=%async_computation.1 | async-start | bytes 1572864 | tf_op jit(solution)/shard_map/all_to_all | solution.py:54
  61.8 0.8 copy.69
  62.9 0.7 bitcast_or_fusion
  63.9 0.8 convert_element_type.36
  64.8 0.2 fusion.8
  65.2 0.4 fusion.5
  66.3 6.8 %gather_fusion.1 = f32[1024]{0:T(1024)S(1)} fusion(f32[128,128]{1,0:T(8,128)S(1)} %exponential_divide_fusion, s32[1024]{0:T(1024)S(1)} %reshape.255), kind=kCustom, calls=%fused_computation.1 | custom fusion | bytes 16384 | tf_op jit(solution)/shard_map/jit(take_along_axis)/gather | solution.py:51
  73.3 74.5 %all-to-all-done.1 = bf16[2,64,12,256]{3,0,2,1:T(2,128)(2,1)S(1)} async-done(((bf16[2,64,12,256]{3,0,2,1:T(2,128)(2,1)}), bf16[2,64,12,256]{3,0,2,1:T(2,128)(2,1)S(1)}, u32[]{:S(2)}, u32[]{:S(2)}) %all-to-all-start.1) | async-done | bytes 786464 | tf_op jit(solution)/shard_map/all_to_all | solution.py:54
  148.2 3.9 %gather_fusion = bf16[1024,256]{1,0:T(8,128)(2,1)S(1)} fusion(bf16[1536,256]{1,0:T(8,128)(2,1)S(1)} %reshape.243, s32[1024]{0:T(1024)S(1)} %broadcast_clamp_fusion), kind=kCustom, calls=%fused_computation | custom fusion | bytes 1052672 | tf_op jit(solution)/shard_map/jit(_take)/gather | solution.py:58
  152.1 0.4 fusion
  152.6 7.2 %psum.14 = f32[128,8]{0,1:T(8,128)S(1)} all-reduce(f32[128,8]{0,1:T(8,128)S(1)} %copy.80), channel_id=1, replica_groups=mesh['ctx_0'=4,'ctx_1'=4,'exp'=64] {'ctx_0'}, use_global_device_ids=true, to_apply=%region_8.9 | all-reduce | flops 1024 | bytes 8192 | tf_op jit(solution)/shard_map/psum | solution.py:23
  159.8 6.3 %psum.15 = f32[128,8]{0,1:T(8,128)S(1)} all-reduce(f32[128,8]{0,1:T(8,128)S(1)} %psum.14), channel_id=1, replica_groups=mesh['ctx_0'=4,'ctx_1'=4,'exp'=64] {'ctx_1'}, use_global_device_ids=true, to_apply=%region_9.10 | all-reduce | flops 1024 | bytes 8192 | tf_op jit(solution)/shard_map/psum | solution.py:23
  166.2 0.3 select_reduce_fusion
  166.6 1.0 convolution_bitcast_fusion
  167.8 5.6 %scatter_custom_fusion = bf16[1536,256]{1,0:T(8,128)(2,1)S(1)} fusion(s32[1024]{0:T(1024)S(1)} %bitcast.46, f32[1024]{0:T(1024)S(1)} %div.58, f32[128,256]{1,0:T(8,128)S(1)} %convert_element_type.36, bf16[]{:T(256)} %constant.73.clone.1), kind=kCustom, calls=%fused_computation.11 | custom fusion | flops 524288 | bytes 921602 | tf_op jit(solution)/shard_map/scatter | solution.py:67
  173.5 0.2 reshape.245
  173.6 1.7 copy.83
  175.3 10.7 %all-to-all-start.2 = ((bf16[2,64,12,256]{3,0,2,1:T(2,128)(2,1)}), bf16[2,64,12,256]{3,0,2,1:T(2,128)(2,1)S(1)}, u32[]{:S(2)}, u32[]{:S(2)}) async-start(bf16[2,64,12,256]{3,0,2,1:T(2,128)(2,1)} %copy.83), calls=%async_computation.2 | async-start | bytes 1572864 | tf_op jit(solution)/shard_map/all_to_all | solution.py:68
  186.1 1.1 multiply_reduce_fusion
  187.2 0.9 convolution_convert_fusion
  188.1 94.1 %all-to-all-done.2 = bf16[2,64,12,256]{3,0,2,1:T(2,128)(2,1)S(1)} async-done(((bf16[2,64,12,256]{3,0,2,1:T(2,128)(2,1)}), bf16[2,64,12,256]{3,0,2,1:T(2,128)(2,1)S(1)}, u32[]{:S(2)}, u32[]{:S(2)}) %all-to-all-start.2) | async-done | bytes 786464 | tf_op jit(solution)/shard_map/all_to_all | solution.py:68
  282.2 1.0 copy.85
  283.2 69.9 %all-gather.3.cloned.1.call-done = f32[16384,128]{0,1:T(8,128)} async-done(((f32[256,128]{0,1:T(8,128)}), f32[16384,128]{0,1:T(8,128)}) %all-gather.3.cloned.1.call-update) | async-done | bytes 8388624 | tf_op jit(solution)/shard_map/all_gather | solution.py:28
  353.1 6.0 %copy.86 = f32[16,8,64,256]{3,2,1,0:T(8,128)S(1)} copy(f32[16,8,64,256]{3,1,2,0:T(8,128)} %bitcast.42) | data formatting | bytes 16777216
  359.1 1.8 bitcast_reduce_fusion
  360.9 0.8 copy.84
  (40 shorter events, 2.5 us)
Async XLA Ops:
  7.2 0.9 copy-start
  7.2 58.5 %copy-start.2 = (s32[128,8]{0,1:T(8,128)S(1)}, s32[128,8]{0,1:T(8,128)}, u32[]{:S(2)}) copy-start(s32[128,8]{0,1:T(8,128)} %param.7) | copy-start | bytes 12292
  10.2 16.3 %all-to-all-start = ((f32[16,128,128]{2,1,0:T(8,128)}), f32[16,128,128]{2,1,0:T(8,128)S(1)}, u32[]{:S(2)}, u32[]{:S(2)}) async-start(f32[16,128,128]{2,1,0:T(8,128)} %broadcast_in_dim.24), calls=%async_computation | async-start | bytes 2097152 | tf_op jit(solution)/shard_map/all_to_all | solution.py:12
  26.6 121.3 %all-to-all-start.1 = ((bf16[2,64,12,256]{3,0,2,1:T(2,128)(2,1)}), bf16[2,64,12,256]{3,0,2,1:T(2,128)(2,1)S(1)}, u32[]{:S(2)}, u32[]{:S(2)}) async-start(bf16[2,64,12,256]{3,0,2,1:T(2,128)(2,1)} %bitcast.4), calls=%async_computation.1 | async-start | bytes 1572864 | tf_op jit(solution)/shard_map/all_to_all | solution.py:54
  61.8 291.3 %all-gather.3.cloned.1.call-start = ((), (), s32[]{:S(2)}) async-start(), calls=%async_computation.3 | async-start | bytes 8519680 | tf_op jit(solution)/shard_map/all_gather | solution.py:28
  73.1 93.5 %copy-start.1 = (bf16[128,256]{1,0:T(8,128)(2,1)S(1)}, bf16[128,256]{1,0:T(8,128)(2,1)}, u32[]{:S(2)}) copy-start(bf16[128,256]{1,0:T(8,128)(2,1)} %param.5) | copy-start | bytes 196612
  175.3 106.9 %all-to-all-start.2 = ((bf16[2,64,12,256]{3,0,2,1:T(2,128)(2,1)}), bf16[2,64,12,256]{3,0,2,1:T(2,128)(2,1)S(1)}, u32[]{:S(2)}, u32[]{:S(2)}) async-start(bf16[2,64,12,256]{3,0,2,1:T(2,128)(2,1)} %copy.83), calls=%async_computation.2 | async-start | bytes 1572864 | tf_op jit(solution)/shard_map/all_to_all | solution.py:68
Sparse Core Ops, SparseCore 0:
  167.7 185.3 all-gather.2
where the time goes:
time: 369 us; the launch traced here: 368 us
  waiting for transfers between devices  245 us (66%)
  starting transfers between devices  52.9 us (14%)
  local copies, waits for them, and re-layouts  27.9 us (8%)
  between operations  14.3 us (4%)
  blocking collectives  13.5 us (4%)
  other arithmetic  11.8 us (3%)
    all_to_all x1, waiting for transfers between devices, body(): lax.all_to_all(weighted_send.reshape(layout), 'exp', split_axis=1, concat...  94.1 us
    all_to_all x1, waiting for transfers between devices, body(): lax.all_to_all(expert_out.reshape(layout), 'exp', split_axis=1, concat_ax...  74.5 us
    all_gather x1, waiting for transfers between devices, gathered_total(): return lax.all_gather(array, axis).sum(0)  69.9 us
    all_to_all x1, starting transfers between devices, body(): lax.all_to_all(expert_out.reshape(layout), 'exp', split_axis=1, concat_ax...  35.2 us
    psum x2, blocking collectives, one_axis_at_a_time(): array = lax.psum(array, axis)  13.5 us
    unnamed x11, local copies, waits for them, and re-layouts  12.2 us
    all_to_all x1, starting transfers between devices, body(): lax.all_to_all(weighted_send.reshape(layout), 'exp', split_axis=1, concat...  10.7 us
  transfers between devices with their start and end apart: 4, of which 4 were waited for; matrix products, arithmetic and copies ran while one was open for 7% of the time, Pallas kernels for 0%

commit v1 on v0

v1 whole, which is shorter than its diff:
```python
import functools

import jax
import jax.numpy as jnp
from jax import lax
from jax.experimental import pallas as pl
from jax.experimental.pallas import tpu as pltpu
from jax.sharding import Mesh
from jax.sharding import PartitionSpec as P


CTX = ("ctx_0", "ctx_1")
NEAR = ("z_lo", "core")
EXP = ("z_hi", "z_lo", "core")
F32 = jnp.float32
BF16 = jnp.bfloat16
INTERPRET = False
NT = (((1,), (1,)), ((), ()))
HIGHEST = lax.Precision.HIGHEST


def broadcast_exchange(array, axes):
    size = lax.axis_size(axes)
    return lax.all_to_all(
        jnp.broadcast_to(array[None], (size, *array.shape)), axes, 0, 0, tiled=True
    )


def ring_parts(array, axis):
    size = lax.axis_size(axis)
    parts = [array]
    for shift in range(1, size):
        parts.append(lax.ppermute(array, axis, [(i, (i + shift) % size) for i in range(size)]))
    return parts


def ring_sum(array, axis):
    parts = ring_parts(array, axis)
    total = parts[0]
    for part in parts[1:]:
        total = total + part
    return total


def split3(x):
    hi = x.astype(BF16)
    rest = x - hi.astype(F32)
    mid = rest.astype(BF16)
    lo = (rest - mid.astype(F32)).astype(BF16)
    return hi, mid, lo


def call(kernel, outs, *args):
    return pl.pallas_call(
        kernel,
        out_shape=[jax.ShapeDtypeStruct(shape, dtype) for shape, dtype in outs],
        interpret=INTERPRET,
    )(*args)


def gate_kernel(logits_ref, routes_ref, cot_ref, probs_ref, small_ref, code_ref, code_t_ref, wt_ref, pay_ref):
    logits = logits_ref[...]
    experts, tokens = logits.shape
    top = routes_ref.shape[0]
    expo = jnp.exp(logits)
    probs = expo / jnp.sum(expo, axis=0, keepdims=True)
    probs_ref[...] = probs
    which = lax.broadcasted_iota(jnp.int32, (experts, tokens), 0)
    hits = [which == routes_ref[k : k + 1, :] for k in range(top)]
    chosen = jnp.concatenate(
        [jnp.sum(jnp.where(hit, probs, 0.0), axis=0, keepdims=True) for hit in hits], axis=0
    )
    total = jnp.sum(chosen, axis=0, keepdims=True)
    gates = chosen / total
    small_ref[0:top, :] = chosen
    small_ref[top : 2 * top, :] = gates
    small_ref[2 * top : 3 * top, :] = jnp.broadcast_to(total, (top, tokens))
    dense = jnp.zeros((experts, tokens), F32)
    member = jnp.zeros((experts, tokens), F32)
    for k in range(top):
        dense = dense + jnp.where(hits[k], gates[k : k + 1, :], 0.0)
        member = member + jnp.where(hits[k], 1.0, 0.0)
    before = lax.broadcasted_iota(jnp.int32, (tokens, tokens), 0)
    after = lax.broadcasted_iota(jnp.int32, (tokens, tokens), 1)
    upper = jnp.where(before < after, 1.0, 0.0).astype(BF16)
    position = jnp.dot(member.astype(BF16), upper, preferred_element_type=F32)
    code = jnp.where(member > 0.5, position, -1.0)
    code_ref[...] = code
    code_t_ref[...] = code.T
    dense_t = dense.T
    for i, term in enumerate(split3(dense_t)):
        wt_ref[i] = term
    pay_ref[0:tokens, :] = cot_ref[...]
    hi, mid, lo = split3(gates)
    names = routes_ref[...].astype(F32)
    extra = jnp.concatenate(
        [
            jnp.concatenate([names, hi.astype(F32)], axis=1),
            jnp.concatenate([mid.astype(F32), lo.astype(F32)], axis=1),
        ],
        axis=0,
    )
    pay_ref[tokens : tokens + 2 * top, :] = extra.astype(BF16)


def combine_kernel(rows_ref, cot_ref, routes_ref, code_ref, code_t_ref, wt_ref, mixed_ref, dots_ref):
    capacity, experts, width = rows_ref.shape
    cot = cot_ref[...]
    code = code_ref[...]
    code_t = code_t_ref[...]
    top, tokens = routes_ref.shape
    dense = jnp.zeros((experts, tokens), F32)
    mixed = jnp.zeros((tokens, width), F32)
    for s in range(capacity):
        rows = rows_ref[s]
        each = lax.dot_general(rows, cot, NT, preferred_element_type=F32)
        dense = dense + jnp.where(code == float(s), each, 0.0)
        here = code_t == float(s)
        for i in range(3):
            weight = jnp.where(here, wt_ref[i].astype(F32), 0.0).astype(BF16)
            mixed = mixed + jnp.dot(weight, rows, preferred_element_type=F32)
    mixed_ref[...] = mixed.astype(BF16)
    which = lax.broadcasted_iota(jnp.int32, (experts, tokens), 0)
    for k in range(top):
        hit = which == routes_ref[k : k + 1, :]
        dots_ref[k : k + 1, :] = jnp.sum(jnp.where(hit, dense, 0.0), axis=0, keepdims=True)


def router_kernel(parts_ref, routes_ref, small_ref, probs_ref, tok_t_ref, part_ref, dlog_ref):
    dots = parts_ref[0]
    for i in range(1, parts_ref.shape[0]):
        dots = dots + parts_ref[i]
    top, _ = dots.shape
    chosen = small_ref[0:top, :]
    gates = small_ref[top : 2 * top, :]
    total = small_ref[2 * top : 3 * top, :]
    dchosen = (dots - jnp.sum(dots * gates, axis=0, keepdims=True)) / total
    level = jnp.sum(chosen * dchosen, axis=0, keepdims=True)
    probs = probs_ref[...]
    which = lax.broadcasted_iota(jnp.int32, probs.shape, 0)
    spread = jnp.zeros(probs.shape, F32)
    for k in range(top):
        spread = spread + jnp.where(which == routes_ref[k : k + 1, :], dchosen[k : k + 1, :], 0.0)
    dlog = probs * (spread - level)
    tok_t = tok_t_ref[...]
    acc = None
    for term in split3(dlog):
        one = lax.dot_general(tok_t, term, NT, preferred_element_type=F32)
        acc = one if acc is None else acc + one
    part_ref[...] = acc
    dlog_ref[...] = dlog


def token_grad_kernel(dlog_ref, weight_ref, out_ref):
    out_ref[...] = lax.dot_general(
        dlog_ref[...].T, weight_ref[...], NT, precision=HIGHEST, preferred_element_type=F32
    ).astype(BF16)


def owner_kernel(group, capacity, local, first_ref, all_ref, out_ref):
    tokens = 128
    top = 8
    height = tokens + 2 * top
    rows = group * capacity
    first = first_ref[0]
    members, weights = [], []
    for q in range(group):
        extra = all_ref[q * height + tokens : (q + 1) * height, :].astype(F32)
        names = extra[0:top, 0:tokens]
        gates = (extra[0:top, tokens:] + extra[top:, 0:tokens]) + extra[top:, tokens:]
        for e in range(local):
            hit = names == (first + e).astype(F32)
            members.append(jnp.sum(jnp.where(hit, 1.0, 0.0), axis=0, keepdims=True))
            weights.append(jnp.sum(jnp.where(hit, gates, 0.0), axis=0, keepdims=True))
    before = lax.broadcasted_iota(jnp.int32, (tokens, tokens), 0)
    after = lax.broadcasted_iota(jnp.int32, (tokens, tokens), 1)
    upper = jnp.where(before < after, 1.0, 0.0).astype(BF16)
    member = jnp.concatenate(members, axis=0)
    position = jnp.dot(member.astype(BF16), upper, preferred_element_type=F32)
    code = jnp.where(member > 0.5, position, -1000.0)
    row = lax.broadcasted_iota(jnp.int32, (rows, tokens), 0).astype(F32)
    picked = jnp.zeros((local * rows, all_ref.shape[1]), F32)
    weight = [jnp.zeros((rows, tokens), F32) for _ in range(local)]
    for q in range(group):
        picks = []
        for e in range(local):
            n = q * local + e
            pick = (code[n : n + 1, :] + float(q * capacity)) == row
            weight[e] = weight[e] + jnp.where(pick, weights[n], 0.0)
            picks.append(jnp.where(pick, 1.0, 0.0))
        select = jnp.concatenate(picks, axis=0).astype(BF16)
        cot = all_ref[q * height : q * height + tokens, :]
        picked = picked + jnp.dot(select, cot, preferred_element_type=F32)
    for e in range(local):
        gate = jnp.sum(weight[e], axis=1, keepdims=True)
        out_ref[e] = (gate * picked[e * rows : (e + 1) * rows, :]).astype(BF16)


def owner_rows(everyone, first, sources, capacity, local):
    group = min(4, sources)
    height = everyone.shape[0] // sources
    width = everyone.shape[1]
    return pl.pallas_call(
        functools.partial(owner_kernel, group, capacity, local),
        grid_spec=pltpu.PrefetchScalarGridSpec(
            num_scalar_prefetch=1,
            grid=(sources // group,),
            in_specs=[pl.BlockSpec((group * height, width), lambda i, first: (i, 0))],
            out_specs=pl.BlockSpec((local, group * capacity, width), lambda i, first: (0, i, 0)),
        ),
        out_shape=jax.ShapeDtypeStruct((local, sources * capacity, width), BF16),
        interpret=INTERPRET,
    )(first, everyone)


def step(tokens, cotangent, routes, router_weight, expert_out):
    rows, top = routes.shape
    local = expert_out.shape[0]
    sources = lax.axis_size(EXP)
    experts = local * sources
    capacity = expert_out.shape[1] // sources
    width = tokens.shape[1]
    routes_t = routes.T

    sent = expert_out.reshape(local, sources, capacity, width).transpose(1, 2, 0, 3)
    returned = lax.all_to_all(sent, EXP, 0, 0, tiled=True)

    partial_logits = lax.dot_general(
        router_weight, tokens.astype(F32), (((0,), (1,)), ((), ())), precision=HIGHEST
    )
    logits = ring_sum(partial_logits, CTX[1])
    logits = ring_sum(logits, CTX[0])
    square = (experts, rows)
    probs, small, code, code_t, wt, payload = call(
        gate_kernel,
        [
            (square, F32),
            ((3 * top, rows), F32),
            (square, F32),
            ((rows, experts), F32),
            ((3, rows, experts), BF16),
            ((rows + 2 * top, width), BF16),
        ],
        logits, routes_t, cotangent,
    )
    everyone = lax.all_gather(payload, EXP, tiled=True)

    arrived = returned.transpose(1, 0, 2, 3).reshape(capacity, experts, width)
    mixed, partial_dots = call(
        combine_kernel,
        [((rows, width), BF16), ((top, rows), F32)],
        arrived, cotangent, routes_t, code, code_t, wt,
    )
    dots = broadcast_exchange(partial_dots, CTX)
    partial_router, dlog = call(
        router_kernel,
        [((width, experts), F32), (square, F32)],
        dots, routes_t, small, probs, tokens.T,
    )
    near = lax.axis_size(NEAR)
    mine = lax.all_to_all(
        partial_router.reshape(near, width // near, experts), NEAR, 0, 0, tiled=True
    ).sum(0)
    mine = broadcast_exchange(mine, "z_hi").sum(0)
    router_grad = broadcast_exchange(mine, NEAR).reshape(width, experts)
    token_grad = call(token_grad_kernel, [((rows, width), BF16)], dlog, router_weight)[0]

    first = (lax.axis_index(EXP) * local).astype(jnp.int32).reshape(1)
    slot_grad = owner_rows(everyone, first, sources, capacity, local)
    return (mixed, token_grad, router_grad, slot_grad)


def solution(mesh):
    n = mesh.shape["exp"]
    side = 4 if mesh.shape["ctx"] == 16 else 2
    low = 4 if n == 64 else 2
    split = Mesh(mesh.devices.reshape(side, -1, n // (2 * low), low, 2), CTX + EXP)
    in_specs = (P(EXP, CTX), P(EXP, CTX), P(EXP, None), P(CTX, None), P(EXP, None, CTX))
    out_specs = (P(EXP, CTX), P(EXP, CTX), P(CTX, None), P(EXP, None, CTX))
    return jax.shard_map(step, mesh=split, in_specs=in_specs, out_specs=out_specs, check_vma=False)
```

time: 369 us -> 263 us (0.71)
  the two profiles are of different devices: /device:TPU:5 before, /device:TPU:1 now
where the time goes in v1:
time: 263 us; the launch traced here: 262 us
  blocking collectives  172 us (65%)
  starting transfers between devices  32.6 us (12%)
  Pallas kernels  20.5 us (8%)
  between operations  14.2 us (5%)
  waiting for transfers between devices  13.7 us (5%)
  local copies, waits for them, and re-layouts  7.8 us (3%)
    all_to_all x1, blocking collectives, step(): returned = lax.all_to_all(sent, EXP, 0, 0, tiled=True)  127 us
    all_to_all x1, blocking collectives, broadcast_exchange(): lax.all_to_all(jnp.broadcast_to(array[None], (size, *array.shape)), axes,...  31.5 us
    ppermute x6, starting transfers between devices, ring_parts(): lax.ppermute(array, axis, [(i, (i + shift) % size) for i in range(size)])  22.1 us
    all_to_all x1, blocking collectives, step(): lax.all_to_all(partial_router.reshape(near, width // near, experts), NEAR...  12.8 us
    pallas_call x1, Pallas kernels, owner_rows(): pl.pallas_call(functools.partial(owner_kernel, group, capacity, local), g...  11.9 us
    all_to_all x2, starting transfers between devices, broadcast_exchange(): lax.all_to_all(jnp.broadcast_to(array[None], (size, *array.shape)), axes,...  10.5 us
    all_to_all x2, waiting for transfers between devices, broadcast_exchange(): lax.all_to_all(jnp.broadcast_to(array[None], (size, *array.shape)), axes,...  9.71 us
    pallas_call x4, Pallas kernels, call(): pl.pallas_call(kernel, out_shape=[jax.ShapeDtypeStruct(shape, dtype) for...  8.56 us
  transfers between devices with their start and end apart: 9, of which 4 were waited for; matrix products, arithmetic and copies ran while one was open for 2% of the time, Pallas kernels for 3%

profile of v1, /device:TPU:1, one launch (start us, length us, event | category | flops | bytes accessed | tf_op | source)
XLA Modules:
  0.0 262.1 jit_solution(2905628779961816927)
XLA Ops:
  7.2 0.0 all-gather.2.cloned.1.call-start
  7.2 1.2 fusion
  8.4 3.9 %collective-permute-start = (f32[128,128]{1,0:T(8,128)S(1)}, f32[128,128]{1,0:T(8,128)S(1)}, u32[]{:S(2)}, u32[]{:S(2)}) collective-permute-start(f32[128,128]{1,0:T(8,128)S(1)} %fusion), channel_id=1, source_target_pairs={{0,64},{64,128},{128,192},{192,0},{1,65},{65,129},{129,193},{193,1... | collective-permute-start | bytes 196616 | tf_op jit(solution)/shard_map/ppermute | solution.py:33
  12.4 4.4 %collective-permute-start.1 = (f32[128,128]{1,0:T(8,128)S(1)}, f32[128,128]{1,0:T(8,128)S(1)}, u32[]{:S(2)}, u32[]{:S(2)}) collective-permute-start(f32[128,128]{1,0:T(8,128)S(1)} %fusion), channel_id=1, source_target_pairs={{0,128},{64,192},{128,0},{192,64},{1,129},{65,193},{129,1},{193,65... | collective-permute-start | bytes 196616 | tf_op jit(solution)/shard_map/ppermute | solution.py:33
  16.7 3.1 %collective-permute-start.2 = (f32[128,128]{1,0:T(8,128)S(1)}, f32[128,128]{1,0:T(8,128)S(1)}, u32[]{:S(2)}, u32[]{:S(2)}) collective-permute-start(f32[128,128]{1,0:T(8,128)S(1)} %fusion), channel_id=1, source_target_pairs={{0,192},{64,0},{128,64},{192,128},{1,193},{65,1},{129,65},{193,129... | collective-permute-start | bytes 196616 | tf_op jit(solution)/shard_map/ppermute | solution.py:33
  19.8 1.9 collective-permute-done.2
  21.8 3.2 %collective-permute-start.3 = (f32[128,128]{1,0:T(8,128)S(1)}, f32[128,128]{1,0:T(8,128)S(1)}, u32[]{:S(2)}, u32[]{:S(2)}) collective-permute-start(f32[128,128]{1,0:T(8,128)S(1)} %add_add_fusion.1), channel_id=1, source_target_pairs={{0,256},{256,512},{512,768},{768,0},{1,257},{257,513},{513,769},{7... | collective-permute-start | bytes 196616 | tf_op jit(solution)/shard_map/ppermute | solution.py:33
  25.0 4.5 %collective-permute-start.4 = (f32[128,128]{1,0:T(8,128)S(1)}, f32[128,128]{1,0:T(8,128)S(1)}, u32[]{:S(2)}, u32[]{:S(2)}) collective-permute-start(f32[128,128]{1,0:T(8,128)S(1)} %add_add_fusion.1), channel_id=1, source_target_pairs={{0,512},{256,768},{512,0},{768,256},{1,513},{257,769},{513,1},{769... | collective-permute-start | bytes 196616 | tf_op jit(solution)/shard_map/ppermute | solution.py:33
  29.5 3.0 %collective-permute-start.5 = (f32[128,128]{1,0:T(8,128)S(1)}, f32[128,128]{1,0:T(8,128)S(1)}, u32[]{:S(2)}, u32[]{:S(2)}) collective-permute-start(f32[128,128]{1,0:T(8,128)S(1)} %add_add_fusion.1), channel_id=1, source_target_pairs={{0,768},{256,0},{512,256},{768,512},{1,769},{257,1},{513,257},{769... | collective-permute-start | bytes 196616 | tf_op jit(solution)/shard_map/ppermute | solution.py:33
  32.5 2.0 collective-permute-done.5
  34.5 0.6 add_add_fusion.logits_ref
  35.2 1.9 shard_map.84
  37.1 0.0 all-gather.2.cloned.1.call-update
  37.1 1.9 copy.14
  39.0 127.2 %all_to_all.25 = bf16[64,12,2,256]{3,2,1,0:T(2,128)(2,1)S(1)} all-to-all(bf16[64,12,2,256]{3,2,1,0:T(2,128)(2,1)S(1)} %bitcast.12), channel_id=1, replica_groups=mesh['ctx_0'=4,'ctx_1'=4,'z_hi'=8,'z_lo'=4,'core'=2] {'z_hi','z_lo','core'}, dimensions={0} | all-to-all | bytes 1572864 | tf_op jit(solution)/shard_map/all_to_all | solution.py:226
  166.2 0.7 copy.15
  166.9 1.2 reshape.27.rows_ref
  168.1 2.9 %shard_map.85 = (bf16[128,256]{1,0:T(8,128)(2,1)}, f32[8,128]{1,0:T(8,128)}) custom-call(bf16[12,128,256]{2,1,0:T(8,128)(2,1)} %reshape.27.rows_ref, bf16[128,256]{1,0:T(8,128)(2,1)} %cot_ref.3, s32[8,128]{1,0:T(8,128)} %bitcast.17, f32[128,128]{1,0:T(8,128)} %get-tuple-element.14.code_ref, f32[128,128]{1,0:T(8,128)} %get-tuple-element.15.code_t_ref, ...), custom_call_target="tpu_custom_call" | custom-call | tf_op jit(solution)/shard_map/pallas_call | solution.py:54
  171.0 1.3 broadcast_in_dim.6
  172.3 5.8 %all-to-all-start.1 = ((f32[16,8,128]{2,1,0:T(8,128)}), f32[16,8,128]{2,1,0:T(8,128)S(1)}, u32[]{:S(2)}, u32[]{:S(2)}) async-start(f32[16,8,128]{2,1,0:T(8,128)} %broadcast_in_dim.6), calls=%async_computation.1 | async-start | bytes 131072 | tf_op jit(solution)/shard_map/all_to_all | solution.py:24
  178.0 0.7 copy.16
  178.8 5.8 %all-to-all-done.1.parts_ref = f32[16,8,128]{2,1,0:T(8,128)S(1)} async-done(((f32[16,8,128]{2,1,0:T(8,128)}), f32[16,8,128]{2,1,0:T(8,128)S(1)}, u32[]{:S(2)}, u32[]{:S(2)}) %all-to-all-start.1) | async-done | bytes 65568 | tf_op jit(solution)/shard_map/all_to_all | solution.py:24
  184.6 0.6 copy-done
  185.2 1.9 shard_map.86
  187.1 12.8 %all_to_all.26 = f32[8,32,128]{2,1,0:T(8,128)S(1)} all-to-all(f32[8,32,128]{2,1,0:T(8,128)} %bitcast.15), channel_id=1, replica_groups=mesh['ctx_0'=4,'ctx_1'=4,'z_hi'=8,'z_lo'=4,'core'=2] {'z_lo','core'}, dimensions={0} | all-to-all | bytes 262144 | tf_op jit(solution)/shard_map/all_to_all | solution.py:261
  199.9 31.5 %all_to_all.27 = f32[8,32,128]{2,1,0:T(8,128)S(1)} all-to-all(f32[8,32,128]{2,1,0:T(8,128)S(1)} %broadcast_in_dim.7), channel_id=1, replica_groups=mesh['ctx_0'=4,'ctx_1'=4,'z_hi'=8,'z_lo'=4,'core'=2] {'z_hi'}, dimensions={0} | all-to-all | bytes 262144 | tf_op jit(solution)/shard_map/all_to_all | solution.py:24
  231.4 0.7 broadcast_in_dim.8
  232.1 4.8 %all-to-all-start.4 = ((f32[8,32,128]{2,1,0:T(8,128)}), f32[8,32,128]{2,1,0:T(8,128)S(1)}, u32[]{:S(2)}, u32[]{:S(2)}) async-start(f32[8,32,128]{2,1,0:T(8,128)} %broadcast_in_dim.8), calls=%async_computation.4 | async-start | bytes 262144 | tf_op jit(solution)/shard_map/all_to_all | solution.py:24
  236.9 1.9 shard_map.87
  238.8 3.9 %all-to-all-done.4 = f32[8,32,128]{2,1,0:T(8,128)S(1)} async-done(((f32[8,32,128]{2,1,0:T(8,128)}), f32[8,32,128]{2,1,0:T(8,128)S(1)}, u32[]{:S(2)}, u32[]{:S(2)}) %all-to-all-start.4) | async-done | bytes 131104 | tf_op jit(solution)/shard_map/all_to_all | solution.py:24
  242.7 11.9 %shard_map.88 = bf16[2,768,256]{2,1,0:T(8,128)(2,1)} custom-call(s32[1]{0:T(128)} %bitcast.7.first_ref, bf16[9216,256]{1,0:T(8,128)(2,1)} %all-gather.2.cloned.1.call-done.all_ref), custom_call_target="tpu_custom_call" | custom-call | tf_op jit(solution)/shard_map/pallas_call | solution.py:203
  254.6 0.7 copy.18
  (12 shorter events, 0.1 us)
Async XLA Ops:
  7.2 170.9 %copy-start.1 = (bf16[128,256]{1,0:T(8,128)(2,1)S(1)}, bf16[128,256]{1,0:T(8,128)(2,1)}, u32[]{:S(2)}) copy-start(bf16[128,256]{1,0:T(8,128)(2,1)} %param.5) | copy-start | bytes 196612
  7.2 235.5 %all-gather.2.cloned.1.call-start = ((), (), s32[]{:S(2)}) async-start(), calls=%async_computation.5 | async-start | bytes 4792320 | tf_op jit(solution)/shard_map/all_gather | solution.py:246
  8.4 11.4 %collective-permute-start = (f32[128,128]{1,0:T(8,128)S(1)}, f32[128,128]{1,0:T(8,128)S(1)}, u32[]{:S(2)}, u32[]{:S(2)}) collective-permute-start(f32[128,128]{1,0:T(8,128)S(1)} %fusion), channel_id=1, source_target_pairs={{0,64},{64,128},{128,192},{192,0},{1,65},{65,129},{129,193},{193,1... | collective-permute-start | bytes 196616 | tf_op jit(solution)/shard_map/ppermute | solution.py:33
  12.4 7.4 %collective-permute-start.1 = (f32[128,128]{1,0:T(8,128)S(1)}, f32[128,128]{1,0:T(8,128)S(1)}, u32[]{:S(2)}, u32[]{:S(2)}) collective-permute-start(f32[128,128]{1,0:T(8,128)S(1)} %fusion), channel_id=1, source_target_pairs={{0,128},{64,192},{128,0},{192,64},{1,129},{65,193},{129,1},{193,65... | collective-permute-start | bytes 196616 | tf_op jit(solution)/shard_map/ppermute | solution.py:33
  16.7 5.0 %collective-permute-start.2 = (f32[128,128]{1,0:T(8,128)S(1)}, f32[128,128]{1,0:T(8,128)S(1)}, u32[]{:S(2)}, u32[]{:S(2)}) collective-permute-start(f32[128,128]{1,0:T(8,128)S(1)} %fusion), channel_id=1, source_target_pairs={{0,192},{64,0},{128,64},{192,128},{1,193},{65,1},{129,65},{193,129... | collective-permute-start | bytes 196616 | tf_op jit(solution)/shard_map/ppermute | solution.py:33
  21.8 10.7 %collective-permute-start.3 = (f32[128,128]{1,0:T(8,128)S(1)}, f32[128,128]{1,0:T(8,128)S(1)}, u32[]{:S(2)}, u32[]{:S(2)}) collective-permute-start(f32[128,128]{1,0:T(8,128)S(1)} %add_add_fusion.1), channel_id=1, source_target_pairs={{0,256},{256,512},{512,768},{768,0},{1,257},{257,513},{513,769},{7... | collective-permute-start | bytes 196616 | tf_op jit(solution)/shard_map/ppermute | solution.py:33
  25.0 7.5 %collective-permute-start.4 = (f32[128,128]{1,0:T(8,128)S(1)}, f32[128,128]{1,0:T(8,128)S(1)}, u32[]{:S(2)}, u32[]{:S(2)}) collective-permute-start(f32[128,128]{1,0:T(8,128)S(1)} %add_add_fusion.1), channel_id=1, source_target_pairs={{0,512},{256,768},{512,0},{768,256},{1,513},{257,769},{513,1},{769... | collective-permute-start | bytes 196616 | tf_op jit(solution)/shard_map/ppermute | solution.py:33
  29.5 5.0 %collective-permute-start.5 = (f32[128,128]{1,0:T(8,128)S(1)}, f32[128,128]{1,0:T(8,128)S(1)}, u32[]{:S(2)}, u32[]{:S(2)}) collective-permute-start(f32[128,128]{1,0:T(8,128)S(1)} %add_add_fusion.1), channel_id=1, source_target_pairs={{0,768},{256,0},{512,256},{768,512},{1,769},{257,1},{513,257},{769... | collective-permute-start | bytes 196616 | tf_op jit(solution)/shard_map/ppermute | solution.py:33
  172.3 12.3 %all-to-all-start.1 = ((f32[16,8,128]{2,1,0:T(8,128)}), f32[16,8,128]{2,1,0:T(8,128)S(1)}, u32[]{:S(2)}, u32[]{:S(2)}) async-start(f32[16,8,128]{2,1,0:T(8,128)} %broadcast_in_dim.6), calls=%async_computation.1 | async-start | bytes 131072 | tf_op jit(solution)/shard_map/all_to_all | solution.py:24
  184.6 0.6 copy-start
  232.1 10.6 %all-to-all-start.4 = ((f32[8,32,128]{2,1,0:T(8,128)}), f32[8,32,128]{2,1,0:T(8,128)S(1)}, u32[]{:S(2)}, u32[]{:S(2)}) async-start(f32[8,32,128]{2,1,0:T(8,128)} %broadcast_in_dim.8), calls=%async_computation.4 | async-start | bytes 262144 | tf_op jit(solution)/shard_map/all_to_all | solution.py:24
Sparse Core Ops, SparseCore 0:
  37.2 195.0 all-gather.1

commit v2 on v1

v2 whole, which is shorter than its diff:
```python
import functools

import jax
import jax.numpy as jnp
import numpy as np
from jax import lax
from jax.experimental import pallas as pl
from jax.experimental.pallas import tpu as pltpu
from jax.sharding import Mesh
from jax.sharding import PartitionSpec as P


CTX = ("ctx_0", "ctx_1")
FAR = "z_hi"
NEAR = ("z_lo", "core")
EXP = ("z_hi", "z_lo", "core")
F32 = jnp.float32
BF16 = jnp.bfloat16
INTERPRET = False
NT = (((1,), (1,)), ((), ()))
HIGHEST = lax.Precision.HIGHEST


def ring_parts(array, axis):
    size = lax.axis_size(axis)
    parts = [array]
    for shift in range(1, size):
        parts.append(lax.ppermute(array, axis, [(i, (i + shift) % size) for i in range(size)]))
    return parts


def ring_sum(array, axis):
    parts = ring_parts(array, axis)
    total = parts[0]
    for part in parts[1:]:
        total = total + part
    return total


def split3(x):
    hi = x.astype(BF16)
    rest = x - hi.astype(F32)
    mid = rest.astype(BF16)
    lo = (rest - mid.astype(F32)).astype(BF16)
    return hi, mid, lo


def call(kernel, outs, *args, vmem=None):
    vmem = vmem or (False,) * len(args)
    return pl.pallas_call(
        kernel,
        out_shape=[jax.ShapeDtypeStruct(shape, dtype) for shape, dtype in outs],
        in_specs=[pl.BlockSpec(memory_space=pltpu.VMEM) for _ in args],
        out_specs=[pl.BlockSpec(memory_space=pltpu.VMEM) for _ in outs],
        interpret=INTERPRET,
    )(*[a if INTERPRET or not v else pltpu.with_memory_space_constraint(a, pltpu.VMEM) for a, v in zip(args, vmem)])


def pack_kernel(perm_ref, in_ref, out_ref):
    local, _, _ = in_ref.shape
    rows = jnp.concatenate([in_ref[e] for e in range(local)], axis=0)
    out = jnp.dot(perm_ref[...], rows, preferred_element_type=F32).astype(BF16)
    out_ref[...] = out.reshape(out_ref.shape)


def pack_rows(expert_out, sources, capacity):
    local, _, width = expert_out.shape
    group = 8
    span = group * capacity
    perm = np.zeros((local * span, local * span), np.float32)
    for s in range(group):
        for e in range(local):
            for c in range(capacity):
                perm[(s * local + e) * capacity + c, e * span + s * capacity + c] = 1.0
    return pl.pallas_call(
        pack_kernel,
        grid=(sources // group,),
        in_specs=[
            pl.BlockSpec((local * span, local * span), lambda i: (0, 0)),
            pl.BlockSpec((local, span, width), lambda i: (0, i, 0)),
        ],
        out_specs=pl.BlockSpec((group, local * capacity, width), lambda i: (i, 0, 0)),
        out_shape=jax.ShapeDtypeStruct((sources, local * capacity, width), BF16),
        interpret=INTERPRET,
    )(jnp.asarray(perm, BF16), expert_out)


def gate_kernel(capacity, logits_ref, routes_ref, probs_ref, small_ref, row_ref, wt_ref, slots_ref):
    logits = logits_ref[...]
    experts, tokens = logits.shape
    top = routes_ref.shape[0]
    expo = jnp.exp(logits)
    probs = expo / jnp.sum(expo, axis=0, keepdims=True)
    probs_ref[...] = probs
    which = lax.broadcasted_iota(jnp.int32, (experts, tokens), 0)
    hits = [which == routes_ref[k : k + 1, :] for k in range(top)]
    chosen = jnp.concatenate(
        [jnp.sum(jnp.where(hit, probs, 0.0), axis=0, keepdims=True) for hit in hits], axis=0
    )
    total = jnp.sum(chosen, axis=0, keepdims=True)
    gates = chosen / total
    small_ref[0:top, :] = chosen
    small_ref[top : 2 * top, :] = gates
    small_ref[2 * top : 3 * top, :] = jnp.broadcast_to(total, (top, tokens))
    dense = jnp.zeros((experts, tokens), F32)
    member = jnp.zeros((experts, tokens), F32)
    for k in range(top):
        dense = dense + jnp.where(hits[k], gates[k : k + 1, :], 0.0)
        member = member + jnp.where(hits[k], 1.0, 0.0)
    before = lax.broadcasted_iota(jnp.int32, (tokens, tokens), 0)
    after = lax.broadcasted_iota(jnp.int32, (tokens, tokens), 1)
    upper = jnp.where(before < after, 1.0, 0.0).astype(BF16)
    position = jnp.dot(member.astype(BF16), upper, preferred_element_type=F32)
    place = which.astype(F32) * float(capacity) + position
    row = jnp.concatenate(
        [jnp.sum(jnp.where(hit, place, 0.0), axis=0, keepdims=True) for hit in hits], axis=0
    )
    row_ref[...] = row
    row_t = row.T
    gates_t = gates.T
    step = min(128, wt_ref.shape[2])
    for c in range(wt_ref.shape[2] // step):
        lane = lax.broadcasted_iota(jnp.int32, (tokens, step), 1).astype(F32) + float(c * step)
        weight = jnp.zeros((tokens, step), F32)
        for k in range(top):
            weight = weight + jnp.where(lane == row_t[:, k : k + 1], gates_t[:, k : k + 1], 0.0)
        for i, term in enumerate(split3(weight)):
            wt_ref[i, :, c * step : (c + 1) * step] = term
    code = jnp.where(member > 0.5, position, -1.0)
    number = after.astype(F32)[0:1, :] + 1.0
    lane = lax.broadcasted_iota(jnp.int32, (experts, 128), 1)
    odd = lax.broadcasted_iota(jnp.int32, (experts, 128), 0) & 1
    lane = lane - 32 * odd
    table = jnp.zeros((experts, 128), F32)
    for s in range(capacity):
        here = code == float(s)
        gate = jnp.sum(jnp.where(here, dense, 0.0), axis=1, keepdims=True)
        token = jnp.sum(jnp.where(here, number, 0.0), axis=1, keepdims=True)
        table = table + jnp.where(lane == s, gate, 0.0) + jnp.where(lane == 16 + s, token, 0.0)
    near, far, _ = slots_ref.shape
    dest = lax.broadcasted_iota(jnp.int32, (near, far, experts), 1) * near
    dest = dest + lax.broadcasted_iota(jnp.int32, (near, far, experts), 0)
    owner = lax.broadcasted_iota(jnp.int32, (near, far, experts), 2) >> 1
    select = jnp.where(dest == owner, 1.0, 0.0).reshape(near * far, experts).astype(BF16)
    slots = sum(jnp.dot(select, term, preferred_element_type=F32) for term in split3(table))
    slots_ref[...] = slots.reshape(near, far, 128)


def combine_kernel(rows_ref, cot_ref, row_ref, wt_ref, mixed_ref, dots_ref):
    sources, each, width = rows_ref.shape
    cot = cot_ref[...]
    top, tokens = row_ref.shape
    mixed = jnp.zeros((tokens, width), F32)
    group = 8
    span = group * each
    acc = [jnp.zeros((8, tokens), F32) for _ in range(top)]
    index = lax.broadcasted_iota(jnp.int32, (span, tokens), 0).astype(F32)
    for c in range(sources // group):
        rows = rows_ref[c * group : (c + 1) * group].reshape(span, width)
        prod = lax.dot_general(rows, cot, NT, preferred_element_type=F32)
        for k in range(top):
            want = row_ref[k : k + 1, :] - float(c * span)
            part = jnp.where(index == want, prod, 0.0)
            acc[k] = acc[k] + jnp.sum(part.reshape(span // 8, 8, tokens), axis=0)
    dots = jnp.concatenate([jnp.sum(a, axis=0, keepdims=True) for a in acc], axis=0)
    for i in range(dots_ref.shape[0]):
        dots_ref[i] = dots
    rows = rows_ref[...].reshape(sources * each, width)
    for i in range(3):
        mixed = mixed + jnp.dot(wt_ref[i], rows, preferred_element_type=F32)
    mixed_ref[...] = mixed.astype(BF16)


def router_kernel(parts_ref, routes_ref, small_ref, probs_ref, tok_t_ref, slots_ref, part_ref, dlog_ref):
    dots = parts_ref[0]
    for i in range(1, parts_ref.shape[0]):
        dots = dots + parts_ref[i]
    top, _ = dots.shape
    chosen = small_ref[0:top, :]
    gates = small_ref[top : 2 * top, :]
    total = small_ref[2 * top : 3 * top, :]
    dchosen = (dots - jnp.sum(dots * gates, axis=0, keepdims=True)) / total
    level = jnp.sum(chosen * dchosen, axis=0, keepdims=True)
    probs = probs_ref[...]
    which = lax.broadcasted_iota(jnp.int32, probs.shape, 0)
    spread = jnp.zeros(probs.shape, F32)
    for k in range(top):
        spread = spread + jnp.where(which == routes_ref[k : k + 1, :], dchosen[k : k + 1, :], 0.0)
    dlog = probs * (spread - level)
    tok_t = tok_t_ref[...]
    acc = None
    for term in split3(dlog):
        one = lax.dot_general(tok_t, term, NT, preferred_element_type=F32)
        acc = one if acc is None else acc + one
    near, far, _ = slots_ref.shape
    share = acc.shape[0] // near
    for n in range(near):
        part_ref[n, 0:share, :] = acc[n * share : (n + 1) * share, :]
        part_ref[n, share : share + far, :] = slots_ref[n]
    dlog_ref[...] = dlog


def near_kernel(in_ref, out_ref):
    near = in_ref.shape[0]
    far = out_ref.shape[0]
    share = in_ref.shape[1] - far
    total = in_ref[0, 0:share, :]
    for n in range(1, near):
        total = total + in_ref[n, 0:share, :]
    for f in range(far):
        out_ref[f, 0:share, :] = total
        for n in range(near):
            out_ref[f, share + n : share + n + 1, :] = in_ref[n, share + f : share + f + 1, :]


def far_kernel(in_ref, out_ref):
    far = in_ref.shape[0]
    share = out_ref.shape[1]
    total = in_ref[0, 0:share, :]
    for f in range(1, far):
        total = total + in_ref[f, 0:share, :]
    for n in range(out_ref.shape[0]):
        out_ref[n] = total


def token_grad_kernel(dlog_ref, weight_ref, out_ref):
    out_ref[...] = lax.dot_general(
        dlog_ref[...].T, weight_ref[...], NT, precision=HIGHEST, preferred_element_type=F32
    ).astype(BF16)


def owner_kernel(capacity, near, tokens, slots_ref, all_ref, out_ref):
    local = out_ref.shape[0]
    share = slots_ref.shape[1] - near
    group = 4
    rows = group * capacity
    index = lax.broadcasted_iota(jnp.int32, (rows, 128), 0)
    source = sum(jnp.where(index >= q * capacity, 1, 0) for q in range(1, group))
    slot = index - capacity * source
    lane = lax.broadcasted_iota(jnp.int32, (rows, 128), 1)
    column = lax.broadcasted_iota(jnp.int32, (rows, group * tokens), 1).astype(F32)
    base = (source[:, 0:1] * tokens).astype(F32)
    for h in range(near // group):
        at = share + h * group
        table = jnp.broadcast_to(slots_ref[0, at : at + 1, :], (rows, 128))
        for q in range(1, group):
            table = jnp.where(source == q, slots_ref[0, at + q : at + q + 1, :], table)
        gates, picks = [], []
        for e in range(local):
            gates.append(jnp.sum(jnp.where(lane == slot + 32 * e, table, 0.0), axis=1, keepdims=True))
            token = jnp.sum(jnp.where(lane == slot + 32 * e + 16, table, 0.0), axis=1, keepdims=True)
            want = jnp.where(token > 0.5, token - 1.0 + base, -1.0)
            picks.append(jnp.where(column == want, 1.0, 0.0).astype(BF16))
        cot = all_ref[h * group * tokens : (h + 1) * group * tokens, :]
        picked = jnp.dot(jnp.concatenate(picks, axis=0), cot, preferred_element_type=F32)
        for e in range(local):
            out_ref[e, h * rows : (h + 1) * rows, :] = (
                gates[e] * picked[e * rows : (e + 1) * rows, :]
            ).astype(BF16)


def owner_rows(everyone, slots, capacity, near, local):
    far, height, _ = slots.shape
    count, width = everyone.shape
    tokens = count // (far * near)
    return pl.pallas_call(
        functools.partial(owner_kernel, capacity, near, tokens),
        grid=(far,),
        in_specs=[
            pl.BlockSpec((1, height, 128), lambda i: (i, 0, 0)),
            pl.BlockSpec((near * tokens, width), lambda i: (i, 0)),
        ],
        out_specs=pl.BlockSpec((local, near * capacity, width), lambda i: (0, i, 0)),
        out_shape=jax.ShapeDtypeStruct((local, far * near * capacity, width), BF16),
        interpret=INTERPRET,
    )(slots, everyone)


def step(tokens, cotangent, routes, router_weight, expert_out):
    rows, top = routes.shape
    local = expert_out.shape[0]
    sources = lax.axis_size(EXP)
    near = lax.axis_size(NEAR)
    far = lax.axis_size(FAR)
    experts = local * sources
    capacity = expert_out.shape[1] // sources
    width = tokens.shape[1]
    share = width // near
    routes_t = routes.T

    everyone = lax.all_gather(cotangent, EXP, tiled=True)
    sent = pack_rows(expert_out, sources, capacity)
    arrived = lax.all_to_all(sent, EXP, 0, 0, tiled=True)

    partial_logits = lax.dot_general(
        router_weight, tokens.astype(F32), (((0,), (1,)), ((), ())), precision=HIGHEST
    )
    logits = ring_sum(partial_logits, CTX[1])
    logits = ring_sum(logits, CTX[0])
    square = (experts, rows)
    probs, small, row, wt, slots = call(
        functools.partial(gate_kernel, capacity),
        [
            (square, F32),
            ((3 * top, rows), F32),
            ((top, rows), F32),
            ((3, rows, experts * capacity), BF16),
            ((near, far, 128), F32),
        ],
        logits, routes_t,
    )

    mixed, partial_dots = call(
        combine_kernel,
        [((rows, width), BF16), ((lax.axis_size(CTX), top, rows), F32)],
        arrived, cotangent, row, wt,
        vmem=(True, False, True, True),
    )
    dots = lax.all_to_all(partial_dots, CTX, 0, 0, tiled=True)
    partial_router, dlog = call(
        router_kernel,
        [((near, share + far, experts), F32), (square, F32)],
        dots, routes_t, small, probs, tokens.T, slots,
        vmem=(True, False, True, True, True, True),
    )
    partial_router = lax.all_to_all(partial_router, NEAR, 0, 0, tiled=True)
    mine = call(near_kernel, [((far, share + near, experts), F32)], partial_router, vmem=(True,))[0]
    mine = lax.all_to_all(mine, FAR, 0, 0, tiled=True)
    total = call(far_kernel, [((near, share, experts), F32)], mine, vmem=(True,))[0]
    router_grad = lax.all_to_all(total, NEAR, 0, 0, tiled=True).reshape(width, experts)
    token_grad = call(token_grad_kernel, [((rows, width), BF16)], dlog, router_weight)[0]
    slot_grad = owner_rows(everyone, mine, capacity, near, local)
    return (mixed, token_grad, router_grad, slot_grad)


def solution(mesh):
    n = mesh.shape["exp"]
    side = 4 if mesh.shape["ctx"] == 16 else 2
    low = 4 if n == 64 else 2
    split = Mesh(mesh.devices.reshape(side, -1, n // (2 * low), low, 2), CTX + EXP)
    in_specs = (P(EXP, CTX), P(EXP, CTX), P(EXP, None), P(CTX, None), P(EXP, None, CTX))
    out_specs = (P(EXP, CTX), P(EXP, CTX), P(CTX, None), P(EXP, None, CTX))
    return jax.shard_map(step, mesh=split, in_specs=in_specs, out_specs=out_specs, check_vma=False)
```

time: 263 us -> 231 us (0.88)
  blocking collectives: 172 us -> 48 us
  waiting for transfers between devices: 13.7 us -> 73.2 us
  starting transfers between devices: 32.6 us -> 64 us
  Pallas kernels: 20.5 us -> 23.7 us
  local copies, waits for them, and re-layouts: 7.8 us -> 5.04 us
    all_to_all x3 -> x2, blocking collectives: 172 us -> 48 us  [the longest x1 35 us: step(): mine = lax.all_to_all(mine, FAR, 0, 0, tiled=True)]
    all_to_all x2 -> x3, waiting for transfers between devices: 9.71 us -> 65.9 us  [the longest x1 59.5 us: step(): arrived = lax.all_to_all(sent, EXP, 0, 0, tiled=True)]
    all_to_all x2 -> x3, starting transfers between devices: 10.5 us -> 42.7 us  [the longest x1 30.4 us: step(): arrived = lax.all_to_all(sent, EXP, 0, 0, tiled=True)]
    pallas_call x4 -> x6, Pallas kernels: 8.56 us -> 11.1 us  [call(): pl.pallas_call(kernel, out_shape=[jax.ShapeDtypeStruct(shape, dtype) for...]
    pallas_call x1 -> x2, Pallas kernels: 11.9 us -> 12.6 us  [the longest x1 6.84 us: owner_rows(): pl.pallas_call(functools.partial(owner_kernel, capacity, near, tokens), g...]
  transfers between devices with their start and end apart: 9 -> 10, of which waited for: 4 -> 5; matrix products, arithmetic and copies ran while one was open for 2% -> 1% of each run, Pallas kernels for 3% -> 8%
where the time goes in v2:
time: 231 us; the launch traced here: 230 us
  waiting for transfers between devices  73.2 us (32%)
  starting transfers between devices  64 us (28%)
  blocking collectives  48 us (21%)
  Pallas kernels  23.7 us (10%)
  between operations  14.2 us (6%)
  local copies, waits for them, and re-layouts  5.04 us (2%)
    all_to_all x1, waiting for transfers between devices, step(): arrived = lax.all_to_all(sent, EXP, 0, 0, tiled=True)  59.5 us
    all_to_all x1, blocking collectives, step(): mine = lax.all_to_all(mine, FAR, 0, 0, tiled=True)  35 us
    all_to_all x1, starting transfers between devices, step(): arrived = lax.all_to_all(sent, EXP, 0, 0, tiled=True)  30.4 us
    ppermute x6, starting transfers between devices, ring_parts(): lax.ppermute(array, axis, [(i, (i + shift) % size) for i in range(size)])  21.3 us
    all_to_all x1, blocking collectives, step(): partial_router = lax.all_to_all(partial_router, NEAR, 0, 0, tiled=True)  13 us
    pallas_call x6, Pallas kernels, call(): pl.pallas_call(kernel, out_shape=[jax.ShapeDtypeStruct(shape, dtype) for...  11.1 us
    pallas_call x1, Pallas kernels, owner_rows(): pl.pallas_call(functools.partial(owner_kernel, capacity, near, tokens), g...  6.84 us
    all_to_all x1, starting transfers between devices, step(): dots = lax.all_to_all(partial_dots, CTX, 0, 0, tiled=True)  6.66 us
  transfers between devices with their start and end apart: 10, of which 5 were waited for; matrix products, arithmetic and copies ran while one was open for 1% of the time, Pallas kernels for 8%

profile of v2, /device:TPU:1, one launch (start us, length us, event | category | flops | bytes accessed | tf_op | source)
XLA Modules:
  0.0 230.0 jit_solution(17748474388730326977)
XLA Ops:
  7.2 5.8 %shard_map.93 = bf16[64,24,256]{2,1,0:T(8,128)(2,1)} custom-call(bf16[192,192]{1,0:T(8,128)(2,1)} %constant.2.clone.perm_ref, bf16[2,768,256]{2,1,0:T(8,128)(2,1)} %in_ref.1), custom_call_target="tpu_custom_call" | custom-call | tf_op jit(solution)/shard_map/pallas_call | solution.py:75
  12.9 30.4 %all-to-all-start = ((bf16[64,24,256]{2,1,0:T(8,128)(2,1)}), bf16[64,24,256]{2,1,0:T(8,128)(2,1)S(1)}, u32[]{:S(2)}, u32[]{:S(2)}) async-start(bf16[64,24,256]{2,1,0:T(8,128)(2,1)} %shard_map.93), calls=%async_computation | async-start | bytes 1572864 | tf_op jit(solution)/shard_map/all_to_all | solution.py:293
  43.4 0.7 all-gather.2.cloned.1.call-update
  44.1 1.2 fusion
  45.3 3.1 %collective-permute-start = (f32[128,128]{1,0:T(8,128)S(1)}, f32[128,128]{1,0:T(8,128)S(1)}, u32[]{:S(2)}, u32[]{:S(2)}) collective-permute-start(f32[128,128]{1,0:T(8,128)S(1)} %fusion), channel_id=1, source_target_pairs={{0,64},{64,128},{128,192},{192,0},{1,65},{65,129},{129,193},{193,1... | collective-permute-start | bytes 196616 | tf_op jit(solution)/shard_map/ppermute | solution.py:28
  48.4 4.4 %collective-permute-start.1 = (f32[128,128]{1,0:T(8,128)S(1)}, f32[128,128]{1,0:T(8,128)S(1)}, u32[]{:S(2)}, u32[]{:S(2)}) collective-permute-start(f32[128,128]{1,0:T(8,128)S(1)} %fusion), channel_id=1, source_target_pairs={{0,128},{64,192},{128,0},{192,64},{1,129},{65,193},{129,1},{193,65... | collective-permute-start | bytes 196616 | tf_op jit(solution)/shard_map/ppermute | solution.py:28
  52.8 3.1 %collective-permute-start.2 = (f32[128,128]{1,0:T(8,128)S(1)}, f32[128,128]{1,0:T(8,128)S(1)}, u32[]{:S(2)}, u32[]{:S(2)}) collective-permute-start(f32[128,128]{1,0:T(8,128)S(1)} %fusion), channel_id=1, source_target_pairs={{0,192},{64,0},{128,64},{192,128},{1,193},{65,1},{129,65},{193,129... | collective-permute-start | bytes 196616 | tf_op jit(solution)/shard_map/ppermute | solution.py:28
  55.8 2.2 collective-permute-done.2
  58.1 3.2 %collective-permute-start.3 = (f32[128,128]{1,0:T(8,128)S(1)}, f32[128,128]{1,0:T(8,128)S(1)}, u32[]{:S(2)}, u32[]{:S(2)}) collective-permute-start(f32[128,128]{1,0:T(8,128)S(1)} %add_add_fusion.1), channel_id=1, source_target_pairs={{0,256},{256,512},{512,768},{768,0},{1,257},{257,513},{513,769},{7... | collective-permute-start | bytes 196616 | tf_op jit(solution)/shard_map/ppermute | solution.py:28
  61.3 4.5 %collective-permute-start.4 = (f32[128,128]{1,0:T(8,128)S(1)}, f32[128,128]{1,0:T(8,128)S(1)}, u32[]{:S(2)}, u32[]{:S(2)}) collective-permute-start(f32[128,128]{1,0:T(8,128)S(1)} %add_add_fusion.1), channel_id=1, source_target_pairs={{0,512},{256,768},{512,0},{768,256},{1,513},{257,769},{513,1},{769... | collective-permute-start | bytes 196616 | tf_op jit(solution)/shard_map/ppermute | solution.py:28
  65.8 3.0 %collective-permute-start.5 = (f32[128,128]{1,0:T(8,128)S(1)}, f32[128,128]{1,0:T(8,128)S(1)}, u32[]{:S(2)}, u32[]{:S(2)}) collective-permute-start(f32[128,128]{1,0:T(8,128)S(1)} %add_add_fusion.1), channel_id=1, source_target_pairs={{0,768},{256,0},{512,256},{768,512},{1,769},{257,1},{513,257},{769... | collective-permute-start | bytes 196616 | tf_op jit(solution)/shard_map/ppermute | solution.py:28
  68.8 2.3 collective-permute-done.5
  71.8 3.9 %shard_map.94 = (f32[128,128]{1,0:T(8,128)}, f32[24,128]{1,0:T(8,128)}, f32[8,128]{1,0:T(8,128)}, bf16[3,128,1536]{2,1,0:T(8,128)(2,1)}, f32[8,8,128]{2,1,0:T(8,128)}) custom-call(f32[128,128]{1,0:T(8,128)} %add_add_fusion.logits_ref, s32[8,128]{1,0:T(8,128)} %bitcast.7), custom_call_target="tpu_custom_call" | custom-call | tf_op jit(solution)/shard_map/pallas_call | solution.py:50
  75.7 59.5 %all-to-all-done.rows_ref = bf16[64,24,256]{2,1,0:T(8,128)(2,1)S(1)} async-done(((bf16[64,24,256]{2,1,0:T(8,128)(2,1)}), bf16[64,24,256]{2,1,0:T(8,128)(2,1)S(1)}, u32[]{:S(2)}, u32[]{:S(2)}) %all-to-all-start) | async-done | bytes 786464 | tf_op jit(solution)/shard_map/all_to_all | solution.py:293
  135.1 1.3 copy-done.1
  136.4 0.7 copy-done.5
  137.1 2.3 %shard_map.95 = (bf16[128,256]{1,0:T(8,128)(2,1)}, f32[16,8,128]{2,1,0:T(8,128)}) custom-call(bf16[64,24,256]{2,1,0:T(8,128)(2,1)S(1)} %all-to-all-done.rows_ref, bf16[128,256]{1,0:T(8,128)(2,1)} %cot_ref.1, f32[8,128]{1,0:T(8,128)S(1)} %copy-done.5, bf16[3,128,1536]{2,1,0:T(8,128)(2,1)S(1)} %copy-done.1), custom_call_target="tpu_custom_call" | custom-call | tf_op jit(solution)/shard_map/pallas_call | solution.py:50
  139.4 6.7 %all-to-all-start.1 = ((f32[16,8,128]{2,1,0:T(8,128)}), f32[16,8,128]{2,1,0:T(8,128)S(1)}, u32[]{:S(2)}, u32[]{:S(2)}) async-start(f32[16,8,128]{2,1,0:T(8,128)} %get-tuple-element.16), calls=%async_computation.1 | async-start | bytes 131072 | tf_op jit(solution)/shard_map/all_to_all | solution.py:319
  146.2 6.4 %all-to-all-done.1.parts_ref = f32[16,8,128]{2,1,0:T(8,128)S(1)} async-done(((f32[16,8,128]{2,1,0:T(8,128)}), f32[16,8,128]{2,1,0:T(8,128)S(1)}, u32[]{:S(2)}, u32[]{:S(2)}) %all-to-all-start.1) | async-done | bytes 65568 | tf_op jit(solution)/shard_map/all_to_all | solution.py:319
  152.6 0.8 copy-done.2
  153.5 0.8 copy-done.3
  154.2 0.7 copy-done.4
  154.9 1.6 shard_map.96
  156.6 13.0 %all_to_all.25.in_ref = f32[8,40,128]{2,1,0:T(8,128)S(1)} all-to-all(f32[8,40,128]{2,1,0:T(8,128)} %get-tuple-element.21), channel_id=1, replica_groups=mesh['ctx_0'=4,'ctx_1'=4,'z_hi'=8,'z_lo'=4,'core'=2] {'z_lo','core'}, dimensions={0} | all-to-all | bytes 327680 | tf_op jit(solution)/shard_map/all_to_all | solution.py:326
  169.5 0.7 shard_map.98
  170.2 35.0 %all_to_all.26.in_ref.slots_ref = f32[8,40,128]{2,1,0:T(8,128)S(1)} all-to-all(f32[8,40,128]{2,1,0:T(8,128)} %shard_map.98), channel_id=1, replica_groups=mesh['ctx_0'=4,'ctx_1'=4,'z_hi'=8,'z_lo'=4,'core'=2] {'z_hi'}, dimensions={0} | all-to-all | bytes 327680 | tf_op jit(solution)/shard_map/all_to_all | solution.py:328
  205.3 0.7 shard_map.99
  206.0 5.7 %all-to-all-start.4 = ((f32[8,32,128]{2,1,0:T(8,128)}), f32[8,32,128]{2,1,0:T(8,128)S(1)}, u32[]{:S(2)}, u32[]{:S(2)}) async-start(f32[8,32,128]{2,1,0:T(8,128)} %shard_map.99), calls=%async_computation.4 | async-start | bytes 262144 | tf_op jit(solution)/shard_map/all_to_all | solution.py:330
  211.7 1.9 shard_map.97
  213.6 2.1 all-gather.2.cloned.1.call-done.all_ref
  215.6 6.8 %shard_map.100 = bf16[2,768,256]{2,1,0:T(8,128)(2,1)} custom-call(f32[8,40,128]{2,1,0:T(8,128)} %copy-done, bf16[8192,256]{1,0:T(8,128)(2,1)} %all-gather.2.cloned.1.call-done.all_ref), custom_call_target="tpu_custom_call" | custom-call | tf_op jit(solution)/shard_map/pallas_call | solution.py:266
  222.5 0.7 copy.12
  (18 shorter events, 0.8 us)
Async XLA Ops:
  7.2 138.9 %copy-start.6 = (bf16[128,256]{1,0:T(8,128)(2,1)S(1)}, bf16[128,256]{1,0:T(8,128)(2,1)}, u32[]{:S(2)}) copy-start(bf16[128,256]{1,0:T(8,128)(2,1)} %param.6) | copy-start | bytes 196612
  12.9 122.2 %all-to-all-start = ((bf16[64,24,256]{2,1,0:T(8,128)(2,1)}), bf16[64,24,256]{2,1,0:T(8,128)(2,1)S(1)}, u32[]{:S(2)}, u32[]{:S(2)}) async-start(bf16[64,24,256]{2,1,0:T(8,128)(2,1)} %shard_map.93), calls=%async_computation | async-start | bytes 1572864 | tf_op jit(solution)/shard_map/all_to_all | solution.py:293
  43.3 172.3 %all-gather.2.cloned.1.call-start = ((), (), s32[]{:S(2)}) async-start(), calls=%async_computation.5 | async-start | bytes 4259840 | tf_op jit(solution)/shard_map/all_gather | solution.py:291
  45.3 10.6 %collective-permute-start = (f32[128,128]{1,0:T(8,128)S(1)}, f32[128,128]{1,0:T(8,128)S(1)}, u32[]{:S(2)}, u32[]{:S(2)}) collective-permute-start(f32[128,128]{1,0:T(8,128)S(1)} %fusion), channel_id=1, source_target_pairs={{0,64},{64,128},{128,192},{192,0},{1,65},{65,129},{129,193},{193,1... | collective-permute-start | bytes 196616 | tf_op jit(solution)/shard_map/ppermute | solution.py:28
  48.4 7.4 %collective-permute-start.1 = (f32[128,128]{1,0:T(8,128)S(1)}, f32[128,128]{1,0:T(8,128)S(1)}, u32[]{:S(2)}, u32[]{:S(2)}) collective-permute-start(f32[128,128]{1,0:T(8,128)S(1)} %fusion), channel_id=1, source_target_pairs={{0,128},{64,192},{128,0},{192,64},{1,129},{65,193},{129,1},{193,65... | collective-permute-start | bytes 196616 | tf_op jit(solution)/shard_map/ppermute | solution.py:28
  52.8 5.3 %collective-permute-start.2 = (f32[128,128]{1,0:T(8,128)S(1)}, f32[128,128]{1,0:T(8,128)S(1)}, u32[]{:S(2)}, u32[]{:S(2)}) collective-permute-start(f32[128,128]{1,0:T(8,128)S(1)} %fusion), channel_id=1, source_target_pairs={{0,192},{64,0},{128,64},{192,128},{1,193},{65,1},{129,65},{193,129... | collective-permute-start | bytes 196616 | tf_op jit(solution)/shard_map/ppermute | solution.py:28
  58.1 10.7 %collective-permute-start.3 = (f32[128,128]{1,0:T(8,128)S(1)}, f32[128,128]{1,0:T(8,128)S(1)}, u32[]{:S(2)}, u32[]{:S(2)}) collective-permute-start(f32[128,128]{1,0:T(8,128)S(1)} %add_add_fusion.1), channel_id=1, source_target_pairs={{0,256},{256,512},{512,768},{768,0},{1,257},{257,513},{513,769},{7... | collective-permute-start | bytes 196616 | tf_op jit(solution)/shard_map/ppermute | solution.py:28
  61.3 7.5 %collective-permute-start.4 = (f32[128,128]{1,0:T(8,128)S(1)}, f32[128,128]{1,0:T(8,128)S(1)}, u32[]{:S(2)}, u32[]{:S(2)}) collective-permute-start(f32[128,128]{1,0:T(8,128)S(1)} %add_add_fusion.1), channel_id=1, source_target_pairs={{0,512},{256,768},{512,0},{768,256},{1,513},{257,769},{513,1},{769... | collective-permute-start | bytes 196616 | tf_op jit(solution)/shard_map/ppermute | solution.py:28
  65.8 5.3 %collective-permute-start.5 = (f32[128,128]{1,0:T(8,128)S(1)}, f32[128,128]{1,0:T(8,128)S(1)}, u32[]{:S(2)}, u32[]{:S(2)}) collective-permute-start(f32[128,128]{1,0:T(8,128)S(1)} %add_add_fusion.1), channel_id=1, source_target_pairs={{0,768},{256,0},{512,256},{768,512},{1,769},{257,1},{513,257},{769... | collective-permute-start | bytes 196616 | tf_op jit(solution)/shard_map/ppermute | solution.py:28
  135.1 1.3 copy-start.1
  136.4 0.7 copy-start.5
  139.4 13.2 %all-to-all-start.1 = ((f32[16,8,128]{2,1,0:T(8,128)}), f32[16,8,128]{2,1,0:T(8,128)S(1)}, u32[]{:S(2)}, u32[]{:S(2)}) async-start(f32[16,8,128]{2,1,0:T(8,128)} %get-tuple-element.16), calls=%async_computation.1 | async-start | bytes 131072 | tf_op jit(solution)/shard_map/all_to_all | solution.py:319
  152.6 0.8 copy-start.2
  153.5 0.8 copy-start.3
  154.2 0.7 copy-start.4
  205.3 10.4 %copy-start = (f32[8,40,128]{2,1,0:T(8,128)}, f32[8,40,128]{2,1,0:T(8,128)S(1)}, u32[]{:S(2)}) copy-start(f32[8,40,128]{2,1,0:T(8,128)S(1)} %all_to_all.26.in_ref.slots_ref) | copy-start | bytes 491524
  206.0 16.5 %all-to-all-start.4 = ((f32[8,32,128]{2,1,0:T(8,128)}), f32[8,32,128]{2,1,0:T(8,128)S(1)}, u32[]{:S(2)}, u32[]{:S(2)}) async-start(f32[8,32,128]{2,1,0:T(8,128)} %shard_map.99), calls=%async_computation.4 | async-start | bytes 262144 | tf_op jit(solution)/shard_map/all_to_all | solution.py:330
Sparse Core Ops, SparseCore 0:
  46.8 168.7 all-gather.1

commit v3 on v2

--- a/solution.py
+++ b/solution.py
@@ -45,22 +45,35 @@
     return hi, mid, lo
 
 
+def near_memory(array):
+    return array if INTERPRET else pltpu.with_memory_space_constraint(array, pltpu.VMEM)
+
+
+def shaped(shape, dtype, vmem):
+    return pltpu.VMEM(shape, dtype) if vmem and not INTERPRET else jax.ShapeDtypeStruct(shape, dtype)
+
+
 def call(kernel, outs, *args, vmem=None):
     vmem = vmem or (False,) * len(args)
     return pl.pallas_call(
         kernel,
-        out_shape=[jax.ShapeDtypeStruct(shape, dtype) for shape, dtype in outs],
+        out_shape=[shaped(*out) for out in outs],
         in_specs=[pl.BlockSpec(memory_space=pltpu.VMEM) for _ in args],
         out_specs=[pl.BlockSpec(memory_space=pltpu.VMEM) for _ in outs],
         interpret=INTERPRET,
-    )(*[a if INTERPRET or not v else pltpu.with_memory_space_constraint(a, pltpu.VMEM) for a, v in zip(args, vmem)])
+    )(*[near_memory(a) if v else a for a, v in zip(args, vmem)])
 
 
 def pack_kernel(perm_ref, in_ref, out_ref):
-    local, _, _ = in_ref.shape
-    rows = jnp.concatenate([in_ref[e] for e in range(local)], axis=0)
-    out = jnp.dot(perm_ref[...], rows, preferred_element_type=F32).astype(BF16)
-    out_ref[...] = out.reshape(out_ref.shape)
+    local, _, width = in_ref.shape
+    dests, each, _ = out_ref.shape
+    span = perm_ref.shape[0] // local
+    group = span * local // each
+    perm = perm_ref[...]
+    for c in range(dests // group):
+        rows = jnp.concatenate([in_ref[e, c * span : (c + 1) * span, :] for e in range(local)], axis=0)
+        out = jnp.dot(perm, rows, preferred_element_type=F32).astype(BF16)
+        out_ref[c * group : (c + 1) * group] = out.reshape(group, each, width)
 
 
 def pack_rows(expert_out, sources, capacity):
@@ -72,17 +85,11 @@
         for e in range(local):
             for c in range(capacity):
                 perm[(s * local + e) * capacity + c, e * span + s * capacity + c] = 1.0
-    return pl.pallas_call(
+    return call(
         pack_kernel,
-        grid=(sources // group,),
-        in_specs=[
-            pl.BlockSpec((local * span, local * span), lambda i: (0, 0)),
-            pl.BlockSpec((local, span, width), lambda i: (0, i, 0)),
-        ],
-        out_specs=pl.BlockSpec((group, local * capacity, width), lambda i: (i, 0, 0)),
-        out_shape=jax.ShapeDtypeStruct((sources, local * capacity, width), BF16),
-        interpret=INTERPRET,
-    )(jnp.asarray(perm, BF16), expert_out)
+        [((sources, local * capacity, width), BF16, True)],
+        jnp.asarray(perm, BF16), expert_out,
+    )[0]
 
 
 def gate_kernel(capacity, logits_ref, routes_ref, probs_ref, small_ref, row_ref, wt_ref, slots_ref):
@@ -230,6 +237,7 @@
 
 
 def owner_kernel(capacity, near, tokens, slots_ref, all_ref, out_ref):
+    step = pl.program_id(0)
     local = out_ref.shape[0]
     share = slots_ref.shape[1] - near
     group = 4
@@ -242,9 +250,9 @@
     base = (source[:, 0:1] * tokens).astype(F32)
     for h in range(near // group):
         at = share + h * group
-        table = jnp.broadcast_to(slots_ref[0, at : at + 1, :], (rows, 128))
+        table = jnp.broadcast_to(slots_ref[step, at : at + 1, :], (rows, 128))
         for q in range(1, group):
-            table = jnp.where(source == q, slots_ref[0, at + q : at + q + 1, :], table)
+            table = jnp.where(source == q, slots_ref[step, at + q : at + q + 1, :], table)
         gates, picks = [], []
         for e in range(local):
             gates.append(jnp.sum(jnp.where(lane == slot + 32 * e, table, 0.0), axis=1, keepdims=True))
@@ -260,20 +268,20 @@
 
 
 def owner_rows(everyone, slots, capacity, near, local):
-    far, height, _ = slots.shape
+    far, _, _ = slots.shape
     count, width = everyone.shape
     tokens = count // (far * near)
     return pl.pallas_call(
         functools.partial(owner_kernel, capacity, near, tokens),
         grid=(far,),
         in_specs=[
-            pl.BlockSpec((1, height, 128), lambda i: (i, 0, 0)),
+            pl.BlockSpec(memory_space=pltpu.VMEM),
             pl.BlockSpec((near * tokens, width), lambda i: (i, 0)),
         ],
         out_specs=pl.BlockSpec((local, near * capacity, width), lambda i: (0, i, 0)),
         out_shape=jax.ShapeDtypeStruct((local, far * near * capacity, width), BF16),
         interpret=INTERPRET,
-    )(slots, everyone)
+    )(near_memory(slots), everyone)
 
 
 def step(tokens, cotangent, routes, router_weight, expert_out):
@@ -301,34 +309,36 @@
     probs, small, row, wt, slots = call(
         functools.partial(gate_kernel, capacity),
         [
-            (square, F32),
-            ((3 * top, rows), F32),
-            ((top, rows), F32),
-            ((3, rows, experts * capacity), BF16),
-            ((near, far, 128), F32),
+            (square, F32, True),
+            ((3 * top, rows), F32, True),
+            ((top, rows), F32, True),
+            ((3, rows, experts * capacity), BF16, True),
+            ((near, far, 128), F32, True),
         ],
         logits, routes_t,
     )
 
     mixed, partial_dots = call(
         combine_kernel,
-        [((rows, width), BF16), ((lax.axis_size(CTX), top, rows), F32)],
+        [((rows, width), BF16, False), ((lax.axis_size(CTX), top, rows), F32, True)],
         arrived, cotangent, row, wt,
         vmem=(True, False, True, True),
     )
     dots = lax.all_to_all(partial_dots, CTX, 0, 0, tiled=True)
     partial_router, dlog = call(
         router_kernel,
-        [((near, share + far, experts), F32), (square, F32)],
+        [((near, share + far, experts), F32, True), (square, F32, True)],
         dots, routes_t, small, probs, tokens.T, slots,
         vmem=(True, False, True, True, True, True),
     )
     partial_router = lax.all_to_all(partial_router, NEAR, 0, 0, tiled=True)
-    mine = call(near_kernel, [((far, share + near, experts), F32)], partial_router, vmem=(True,))[0]
+    mine = call(near_kernel, [((far, share + near, experts), F32, True)], partial_router, vmem=(True,))[0]
     mine = lax.all_to_all(mine, FAR, 0, 0, tiled=True)
-    total = call(far_kernel, [((near, share, experts), F32)], mine, vmem=(True,))[0]
+    total = call(far_kernel, [((near, share, experts), F32, True)], mine, vmem=(True,))[0]
     router_grad = lax.all_to_all(total, NEAR, 0, 0, tiled=True).reshape(width, experts)
-    token_grad = call(token_grad_kernel, [((rows, width), BF16)], dlog, router_weight)[0]
+    token_grad = call(
+        token_grad_kernel, [((rows, width), BF16, False)], dlog, router_weight, vmem=(True, False)
+    )[0]
     slot_grad = owner_rows(everyone, mine, capacity, near, local)
     return (mixed, token_grad, router_grad, slot_grad)
 

time: 231 us -> 227 us (0.983)
  the two profiles are of different devices: /device:TPU:1 before, /device:TPU:25 now
where the time goes in v3:
time: 227 us; the launch traced here: 226 us
  waiting for transfers between devices  82.1 us (36%)
  starting transfers between devices  61.9 us (27%)
  blocking collectives  46.8 us (21%)
  Pallas kernels  18.3 us (8%)
  between operations  14.2 us (6%)
    all_to_all x1, waiting for transfers between devices, step(): arrived = lax.all_to_all(sent, EXP, 0, 0, tiled=True)  60.4 us
    all_to_all x1, blocking collectives, step(): mine = lax.all_to_all(mine, FAR, 0, 0, tiled=True)  34.7 us
    all_to_all x1, starting transfers between devices, step(): arrived = lax.all_to_all(sent, EXP, 0, 0, tiled=True)  29.6 us
    ppermute x6, starting transfers between devices, ring_parts(): lax.ppermute(array, axis, [(i, (i + shift) % size) for i in range(size)])  18.5 us
    all_to_all x1, blocking collectives, step(): partial_router = lax.all_to_all(partial_router, NEAR, 0, 0, tiled=True)  12.1 us
    pallas_call x7, Pallas kernels, call(): pl.pallas_call(kernel, out_shape=[shaped(*out) for out in outs], in_specs...  11.6 us
    all_gather x1, waiting for transfers between devices, step(): everyone = lax.all_gather(cotangent, EXP, tiled=True)  9.48 us
    all_to_all x1, starting transfers between devices, step(): lax.all_to_all(total, NEAR, 0, 0, tiled=True).reshape(width, experts)  7.08 us
  transfers between devices with their start and end apart: 10, of which 6 were waited for; matrix products, arithmetic and copies ran while one was open for 1% of the time, Pallas kernels for 7%

profile of v3, /device:TPU:25, one launch (start us, length us, event | category | flops | bytes accessed | tf_op | source)
XLA Modules:
  0.0 225.9 jit_solution(15002226416914744998)
XLA Ops:
  7.2 0.0 copy-start
  7.2 2.5 %shard_map.93 = bf16[64,24,256]{2,1,0:T(8,128)(2,1)} custom-call(bf16[192,192]{1,0:T(8,128)(2,1)} %constant.2.clone.perm_ref, bf16[2,768,256]{2,1,0:T(8,128)(2,1)} %in_ref.1), custom_call_target="tpu_custom_call" | custom-call | tf_op jit(solution)/shard_map/pallas_call | solution.py:58
  9.6 29.6 %all-to-all-start = ((bf16[64,24,256]{2,1,0:T(8,128)(2,1)}), bf16[64,24,256]{2,1,0:T(8,128)(2,1)S(1)}, u32[]{:S(2)}, u32[]{:S(2)}) async-start(bf16[64,24,256]{2,1,0:T(8,128)(2,1)} %shard_map.93), calls=%async_computation | async-start | bytes 1572864 | tf_op jit(solution)/shard_map/all_to_all | solution.py:301
  39.2 0.0 all-gather.2.cloned.1.call-start
  39.3 0.7 all-gather.2.cloned.1.call-update
  40.0 1.2 fusion
  41.1 3.1 %collective-permute-start = (f32[128,128]{1,0:T(8,128)S(1)}, f32[128,128]{1,0:T(8,128)S(1)}, u32[]{:S(2)}, u32[]{:S(2)}) collective-permute-start(f32[128,128]{1,0:T(8,128)S(1)} %fusion), channel_id=1, source_target_pairs={{0,64},{64,128},{128,192},{192,0},{1,65},{65,129},{129,193},{193,1... | collective-permute-start | bytes 196616 | tf_op jit(solution)/shard_map/ppermute | solution.py:28
  44.3 4.4 %collective-permute-start.1 = (f32[128,128]{1,0:T(8,128)S(1)}, f32[128,128]{1,0:T(8,128)S(1)}, u32[]{:S(2)}, u32[]{:S(2)}) collective-permute-start(f32[128,128]{1,0:T(8,128)S(1)} %fusion), channel_id=1, source_target_pairs={{0,128},{64,192},{128,0},{192,64},{1,129},{65,193},{129,1},{193,65... | collective-permute-start | bytes 196616 | tf_op jit(solution)/shard_map/ppermute | solution.py:28
  48.6 3.1 %collective-permute-start.2 = (f32[128,128]{1,0:T(8,128)S(1)}, f32[128,128]{1,0:T(8,128)S(1)}, u32[]{:S(2)}, u32[]{:S(2)}) collective-permute-start(f32[128,128]{1,0:T(8,128)S(1)} %fusion), channel_id=1, source_target_pairs={{0,192},{64,0},{128,64},{192,128},{1,193},{65,1},{129,65},{193,129... | collective-permute-start | bytes 196616 | tf_op jit(solution)/shard_map/ppermute | solution.py:28
  51.7 0.0 collective-permute-done
  51.7 2.2 collective-permute-done.2
  54.0 1.9 collective-permute-start.3
  55.9 4.1 %collective-permute-start.4 = (f32[128,128]{1,0:T(8,128)S(1)}, f32[128,128]{1,0:T(8,128)S(1)}, u32[]{:S(2)}, u32[]{:S(2)}) collective-permute-start(f32[128,128]{1,0:T(8,128)S(1)} %add_add_fusion.1), channel_id=1, source_target_pairs={{0,512},{256,768},{512,0},{768,256},{1,513},{257,769},{513,1},{769... | collective-permute-start | bytes 196616 | tf_op jit(solution)/shard_map/ppermute | solution.py:28
  60.0 1.9 collective-permute-start.5
  62.0 0.7 collective-permute-done.4
  62.7 3.9 %collective-permute-done.5 = f32[128,128]{1,0:T(8,128)S(1)} collective-permute-done((f32[128,128]{1,0:T(8,128)S(1)}, f32[128,128]{1,0:T(8,128)S(1)}, u32[]{:S(2)}, u32[]{:S(2)}) %collective-permute-start.5) | collective-permute-done | bytes 65568 | tf_op jit(solution)/shard_map/ppermute | solution.py:28
  66.6 0.6 add_add_fusion.logits_ref
  67.2 3.2 %shard_map.94 = (f32[128,128]{1,0:T(8,128)S(1)}, f32[24,128]{1,0:T(8,128)S(1)}, f32[8,128]{1,0:T(8,128)S(1)}, bf16[3,128,1536]{2,1,0:T(8,128)(2,1)S(1)}, f32[8,8,128]{2,1,0:T(8,128)S(1)}) custom-call(f32[128,128]{1,0:T(8,128)} %add_add_fusion.logits_ref, s32[8,128]{1,0:T(8,128)} %bitcast.7), custom_call_target="tpu_custom_call" | custom-call | tf_op jit(solution)/shard_map/pallas_call | solution.py:58
  70.5 60.4 %all-to-all-done.rows_ref = bf16[64,24,256]{2,1,0:T(8,128)(2,1)S(1)} async-done(((bf16[64,24,256]{2,1,0:T(8,128)(2,1)}), bf16[64,24,256]{2,1,0:T(8,128)(2,1)S(1)}, u32[]{:S(2)}, u32[]{:S(2)}) %all-to-all-start) | async-done | bytes 786464 | tf_op jit(solution)/shard_map/all_to_all | solution.py:301
  130.9 2.3 %shard_map.95 = (bf16[128,256]{1,0:T(8,128)(2,1)}, f32[16,8,128]{2,1,0:T(8,128)}) custom-call(bf16[64,24,256]{2,1,0:T(8,128)(2,1)S(1)} %all-to-all-done.rows_ref, bf16[128,256]{1,0:T(8,128)(2,1)} %cot_ref.1, f32[8,128]{1,0:T(8,128)S(1)} %get-tuple-element.13.row_ref, bf16[3,128,1536]{2,1,0:T(8,128)(2,1)S(1)} %get-tuple-element.14.wt_ref), custom_call_target="tpu_custom_call" | custom-call | tf_op jit(solution)/shard_map/pallas_call | solution.py:58
  133.2 6.7 %all-to-all-start.1 = ((f32[16,8,128]{2,1,0:T(8,128)}), f32[16,8,128]{2,1,0:T(8,128)S(1)}, u32[]{:S(2)}, u32[]{:S(2)}) async-start(f32[16,8,128]{2,1,0:T(8,128)} %get-tuple-element.16), calls=%async_computation.1 | async-start | bytes 131072 | tf_op jit(solution)/shard_map/all_to_all | solution.py:327
  139.9 0.1 copy.10
  140.0 4.7 %all-to-all-done.1.parts_ref = f32[16,8,128]{2,1,0:T(8,128)S(1)} async-done(((f32[16,8,128]{2,1,0:T(8,128)}), f32[16,8,128]{2,1,0:T(8,128)S(1)}, u32[]{:S(2)}, u32[]{:S(2)}) %all-to-all-start.1) | async-done | bytes 65568 | tf_op jit(solution)/shard_map/all_to_all | solution.py:327
  144.7 1.0 shard_map.96
  145.7 12.1 %all_to_all.25.in_ref = f32[8,40,128]{2,1,0:T(8,128)S(1)} all-to-all(f32[8,40,128]{2,1,0:T(8,128)S(1)} %get-tuple-element.21), channel_id=1, replica_groups=mesh['ctx_0'=4,'ctx_1'=4,'z_hi'=8,'z_lo'=4,'core'=2] {'z_lo','core'}, dimensions={0} | all-to-all | bytes 327680 | tf_op jit(solution)/shard_map/all_to_all | solution.py:334
  157.8 34.7 %all_to_all.26.in_ref.slots_ref = f32[8,40,128]{2,1,0:T(8,128)S(1)} all-to-all(f32[8,40,128]{2,1,0:T(8,128)S(1)} %shard_map.98), channel_id=1, replica_groups=mesh['ctx_0'=4,'ctx_1'=4,'z_hi'=8,'z_lo'=4,'core'=2] {'z_hi'}, dimensions={0} | all-to-all | bytes 327680 | tf_op jit(solution)/shard_map/all_to_all | solution.py:336
  192.5 0.7 shard_map.99
  193.2 7.1 %all-to-all-start.4 = ((f32[8,32,128]{2,1,0:T(8,128)}), f32[8,32,128]{2,1,0:T(8,128)S(1)}, u32[]{:S(2)}, u32[]{:S(2)}) async-start(f32[8,32,128]{2,1,0:T(8,128)} %shard_map.99), calls=%async_computation.4 | async-start | bytes 262144 | tf_op jit(solution)/shard_map/all_to_all | solution.py:338
  200.2 1.9 shard_map.97
  202.1 9.5 %all-gather.2.cloned.1.call-done.all_ref = bf16[8192,256]{1,0:T(8,128)(2,1)} async-done(((bf16[128,256]{1,0:T(8,128)(2,1)}), bf16[8192,256]{1,0:T(8,128)(2,1)}) %all-gather.2.cloned.1.call-update) | async-done | bytes 4194320 | tf_op jit(solution)/shard_map/all_gather | solution.py:299
  211.6 6.8 %shard_map.100 = bf16[2,768,256]{2,1,0:T(8,128)(2,1)} custom-call(f32[8,40,128]{2,1,0:T(8,128)S(1)} %all_to_all.26.in_ref.slots_ref, bf16[8192,256]{1,0:T(8,128)(2,1)} %all-gather.2.cloned.1.call-done.all_ref), custom_call_target="tpu_custom_call" | custom-call | tf_op jit(solution)/shard_map/pallas_call | solution.py:274
  218.4 0.7 copy.12
  (6 shorter events, 0.1 us)
Async XLA Ops:
  7.2 132.7 %copy-start = (bf16[128,256]{1,0:T(8,128)(2,1)S(1)}, bf16[128,256]{1,0:T(8,128)(2,1)}, u32[]{:S(2)}) copy-start(bf16[128,256]{1,0:T(8,128)(2,1)} %param.6) | copy-start | bytes 196612
  9.6 121.2 %all-to-all-start = ((bf16[64,24,256]{2,1,0:T(8,128)(2,1)}), bf16[64,24,256]{2,1,0:T(8,128)(2,1)S(1)}, u32[]{:S(2)}, u32[]{:S(2)}) async-start(bf16[64,24,256]{2,1,0:T(8,128)(2,1)} %shard_map.93), calls=%async_computation | async-start | bytes 1572864 | tf_op jit(solution)/shard_map/all_to_all | solution.py:301
  39.2 172.4 %all-gather.2.cloned.1.call-start = ((), (), s32[]{:S(2)}) async-start(), calls=%async_computation.5 | async-start | bytes 4259840 | tf_op jit(solution)/shard_map/all_gather | solution.py:299
  41.1 10.6 %collective-permute-start = (f32[128,128]{1,0:T(8,128)S(1)}, f32[128,128]{1,0:T(8,128)S(1)}, u32[]{:S(2)}, u32[]{:S(2)}) collective-permute-start(f32[128,128]{1,0:T(8,128)S(1)} %fusion), channel_id=1, source_target_pairs={{0,64},{64,128},{128,192},{192,0},{1,65},{65,129},{129,193},{193,1... | collective-permute-start | bytes 196616 | tf_op jit(solution)/shard_map/ppermute | solution.py:28
  44.3 7.5 %collective-permute-start.1 = (f32[128,128]{1,0:T(8,128)S(1)}, f32[128,128]{1,0:T(8,128)S(1)}, u32[]{:S(2)}, u32[]{:S(2)}) collective-permute-start(f32[128,128]{1,0:T(8,128)S(1)} %fusion), channel_id=1, source_target_pairs={{0,128},{64,192},{128,0},{192,64},{1,129},{65,193},{129,1},{193,65... | collective-permute-start | bytes 196616 | tf_op jit(solution)/shard_map/ppermute | solution.py:28
  48.6 5.3 %collective-permute-start.2 = (f32[128,128]{1,0:T(8,128)S(1)}, f32[128,128]{1,0:T(8,128)S(1)}, u32[]{:S(2)}, u32[]{:S(2)}) collective-permute-start(f32[128,128]{1,0:T(8,128)S(1)} %fusion), channel_id=1, source_target_pairs={{0,192},{64,0},{128,64},{192,128},{1,193},{65,1},{129,65},{193,129... | collective-permute-start | bytes 196616 | tf_op jit(solution)/shard_map/ppermute | solution.py:28
  54.0 8.0 %collective-permute-start.3 = (f32[128,128]{1,0:T(8,128)S(1)}, f32[128,128]{1,0:T(8,128)S(1)}, u32[]{:S(2)}, u32[]{:S(2)}) collective-permute-start(f32[128,128]{1,0:T(8,128)S(1)} %add_add_fusion.1), channel_id=1, source_target_pairs={{0,256},{256,512},{512,768},{768,0},{1,257},{257,513},{513,769},{7... | collective-permute-start | bytes 196616 | tf_op jit(solution)/shard_map/ppermute | solution.py:28
  55.9 6.8 %collective-permute-start.4 = (f32[128,128]{1,0:T(8,128)S(1)}, f32[128,128]{1,0:T(8,128)S(1)}, u32[]{:S(2)}, u32[]{:S(2)}) collective-permute-start(f32[128,128]{1,0:T(8,128)S(1)} %add_add_fusion.1), channel_id=1, source_target_pairs={{0,512},{256,768},{512,0},{768,256},{1,513},{257,769},{513,1},{769... | collective-permute-start | bytes 196616 | tf_op jit(solution)/shard_map/ppermute | solution.py:28
  60.0 6.5 %collective-permute-start.5 = (f32[128,128]{1,0:T(8,128)S(1)}, f32[128,128]{1,0:T(8,128)S(1)}, u32[]{:S(2)}, u32[]{:S(2)}) collective-permute-start(f32[128,128]{1,0:T(8,128)S(1)} %add_add_fusion.1), channel_id=1, source_target_pairs={{0,768},{256,0},{512,256},{768,512},{1,769},{257,1},{513,257},{769... | collective-permute-start | bytes 196616 | tf_op jit(solution)/shard_map/ppermute | solution.py:28
  133.2 11.5 %all-to-all-start.1 = ((f32[16,8,128]{2,1,0:T(8,128)}), f32[16,8,128]{2,1,0:T(8,128)S(1)}, u32[]{:S(2)}, u32[]{:S(2)}) async-start(f32[16,8,128]{2,1,0:T(8,128)} %get-tuple-element.16), calls=%async_computation.1 | async-start | bytes 131072 | tf_op jit(solution)/shard_map/all_to_all | solution.py:327
  193.2 25.2 %all-to-all-start.4 = ((f32[8,32,128]{2,1,0:T(8,128)}), f32[8,32,128]{2,1,0:T(8,128)S(1)}, u32[]{:S(2)}, u32[]{:S(2)}) async-start(f32[8,32,128]{2,1,0:T(8,128)} %shard_map.99), calls=%async_computation.4 | async-start | bytes 262144 | tf_op jit(solution)/shard_map/all_to_all | solution.py:338
Sparse Core Ops, SparseCore 0:
  42.7 168.8 all-gather.1

commit v4 on v3

--- a/solution.py
+++ b/solution.py
@@ -14,6 +14,7 @@
 FAR = "z_hi"
 NEAR = ("z_lo", "core")
 EXP = ("z_hi", "z_lo", "core")
+SPREAD = ("z_lo", "z_hi", "core")
 F32 = jnp.float32
 BF16 = jnp.bfloat16
 INTERPRET = False
@@ -73,12 +74,14 @@
     for c in range(dests // group):
         rows = jnp.concatenate([in_ref[e, c * span : (c + 1) * span, :] for e in range(local)], axis=0)
         out = jnp.dot(perm, rows, preferred_element_type=F32).astype(BF16)
-        out_ref[c * group : (c + 1) * group] = out.reshape(group, each, width)
-
-
-def pack_rows(expert_out, sources, capacity):
+        out = out.reshape(group, each, width)
+        for low in range(group // 2):
+            at = low * 2 * (dests // group) + 2 * c
+            out_ref[at : at + 2] = out[2 * low : 2 * low + 2]
+
+
+def pack_rows(expert_out, sources, capacity, group):
     local, _, width = expert_out.shape
-    group = 8
     span = group * capacity
     perm = np.zeros((local * span, local * span), np.float32)
     for s in range(group):
@@ -118,7 +121,11 @@
     after = lax.broadcasted_iota(jnp.int32, (tokens, tokens), 1)
     upper = jnp.where(before < after, 1.0, 0.0).astype(BF16)
     position = jnp.dot(member.astype(BF16), upper, preferred_element_type=F32)
-    place = which.astype(F32) * float(capacity) + position
+    near, far, _ = slots_ref.shape
+    span = experts // far
+    high, rest = which // span, which % span
+    order = (rest // 4) * (4 * far) + high * 4 + rest % 4
+    place = order.astype(F32) * float(capacity) + position
     row = jnp.concatenate(
         [jnp.sum(jnp.where(hit, place, 0.0), axis=0, keepdims=True) for hit in hits], axis=0
     )
@@ -144,7 +151,6 @@
         gate = jnp.sum(jnp.where(here, dense, 0.0), axis=1, keepdims=True)
         token = jnp.sum(jnp.where(here, number, 0.0), axis=1, keepdims=True)
         table = table + jnp.where(lane == s, gate, 0.0) + jnp.where(lane == 16 + s, token, 0.0)
-    near, far, _ = slots_ref.shape
     dest = lax.broadcasted_iota(jnp.int32, (near, far, experts), 1) * near
     dest = dest + lax.broadcasted_iota(jnp.int32, (near, far, experts), 0)
     owner = lax.broadcasted_iota(jnp.int32, (near, far, experts), 2) >> 1
@@ -153,11 +159,10 @@
     slots_ref[...] = slots.reshape(near, far, 128)
 
 
-def combine_kernel(rows_ref, cot_ref, row_ref, wt_ref, mixed_ref, dots_ref):
+def dots_kernel(rows_ref, cot_ref, row_ref, dots_ref):
     sources, each, width = rows_ref.shape
     cot = cot_ref[...]
     top, tokens = row_ref.shape
-    mixed = jnp.zeros((tokens, width), F32)
     group = 8
     span = group * each
     acc = [jnp.zeros((8, tokens), F32) for _ in range(top)]
@@ -172,8 +177,13 @@
     dots = jnp.concatenate([jnp.sum(a, axis=0, keepdims=True) for a in acc], axis=0)
     for i in range(dots_ref.shape[0]):
         dots_ref[i] = dots
+
+
+def mixed_kernel(rows_ref, wt_ref, mixed_ref):
+    sources, each, width = rows_ref.shape
     rows = rows_ref[...].reshape(sources * each, width)
-    for i in range(3):
+    mixed = jnp.dot(wt_ref[0], rows, preferred_element_type=F32)
+    for i in range(1, 3):
         mixed = mixed + jnp.dot(wt_ref[i], rows, preferred_element_type=F32)
     mixed_ref[...] = mixed.astype(BF16)
 
@@ -236,8 +246,7 @@
     ).astype(BF16)
 
 
-def owner_kernel(capacity, near, tokens, slots_ref, all_ref, out_ref):
-    step = pl.program_id(0)
+def owner_kernel(capacity, near, tokens, pair, slots_ref, all_ref, out_ref):
     local = out_ref.shape[0]
     share = slots_ref.shape[1] - near
     group = 4
@@ -248,8 +257,9 @@
     lane = lax.broadcasted_iota(jnp.int32, (rows, 128), 1)
     column = lax.broadcasted_iota(jnp.int32, (rows, group * tokens), 1).astype(F32)
     base = (source[:, 0:1] * tokens).astype(F32)
-    for h in range(near // group):
-        at = share + h * group
+    for h in range(pair * near // group):
+        step = pl.program_id(0) * pair + h * group // near
+        at = share + h * group % near
         table = jnp.broadcast_to(slots_ref[step, at : at + 1, :], (rows, 128))
         for q in range(1, group):
             table = jnp.where(source == q, slots_ref[step, at + q : at + q + 1, :], table)
@@ -268,17 +278,18 @@
 
 
 def owner_rows(everyone, slots, capacity, near, local):
-    far, _, _ = slots.shape
+    far = slots.shape[0]
     count, width = everyone.shape
     tokens = count // (far * near)
+    pair = 2
     return pl.pallas_call(
-        functools.partial(owner_kernel, capacity, near, tokens),
-        grid=(far,),
+        functools.partial(owner_kernel, capacity, near, tokens, pair),
+        grid=(far // pair,),
         in_specs=[
             pl.BlockSpec(memory_space=pltpu.VMEM),
-            pl.BlockSpec((near * tokens, width), lambda i: (i, 0)),
+            pl.BlockSpec((pair * near * tokens, width), lambda i: (i, 0)),
         ],
-        out_specs=pl.BlockSpec((local, near * capacity, width), lambda i: (0, i, 0)),
+        out_specs=pl.BlockSpec((local, pair * near * capacity, width), lambda i: (0, i, 0)),
         out_shape=jax.ShapeDtypeStruct((local, far * near * capacity, width), BF16),
         interpret=INTERPRET,
     )(near_memory(slots), everyone)
@@ -297,8 +308,8 @@
     routes_t = routes.T
 
     everyone = lax.all_gather(cotangent, EXP, tiled=True)
-    sent = pack_rows(expert_out, sources, capacity)
-    arrived = lax.all_to_all(sent, EXP, 0, 0, tiled=True)
+    sent = pack_rows(expert_out, sources, capacity, near)
+    arrived = lax.all_to_all(sent, SPREAD, 0, 0, tiled=True)
 
     partial_logits = lax.dot_general(
         router_weight, tokens.astype(F32), (((0,), (1,)), ((), ())), precision=HIGHEST
@@ -312,19 +323,20 @@
             (square, F32, True),
             ((3 * top, rows), F32, True),
             ((top, rows), F32, True),
-            ((3, rows, experts * capacity), BF16, True),
+            ((3, rows, experts * capacity), BF16, False),
             ((near, far, 128), F32, True),
         ],
         logits, routes_t,
     )
 
-    mixed, partial_dots = call(
-        combine_kernel,
-        [((rows, width), BF16, False), ((lax.axis_size(CTX), top, rows), F32, True)],
-        arrived, cotangent, row, wt,
-        vmem=(True, False, True, True),
-    )
+    partial_dots = call(
+        dots_kernel,
+        [((lax.axis_size(CTX), top, rows), F32, True)],
+        arrived, cotangent, row,
+        vmem=(True, False, True),
+    )[0]
     dots = lax.all_to_all(partial_dots, CTX, 0, 0, tiled=True)
+    mixed = call(mixed_kernel, [((rows, width), BF16, False)], arrived, wt, vmem=(True, False))[0]
     partial_router, dlog = call(
         router_kernel,
         [((near, share + far, experts), F32, True), (square, F32, True)],

time: 227 us -> 226 us (level)
  the two profiles are of different devices: /device:TPU:25 before, /device:TPU:5 now
where the time goes in v4:
time: 226 us; the launch traced here: 225 us
  waiting for transfers between devices  77.5 us (34%)
  starting transfers between devices  61.4 us (27%)
  blocking collectives  50 us (22%)
  Pallas kernels  19 us (8%)
  between operations  14.1 us (6%)
    all_to_all x1, waiting for transfers between devices, step(): arrived = lax.all_to_all(sent, SPREAD, 0, 0, tiled=True)  58 us
    all_to_all x1, blocking collectives, step(): mine = lax.all_to_all(mine, FAR, 0, 0, tiled=True)  39.5 us
    all_to_all x1, starting transfers between devices, step(): arrived = lax.all_to_all(sent, SPREAD, 0, 0, tiled=True)  29.6 us
    ppermute x6, starting transfers between devices, ring_parts(): lax.ppermute(array, axis, [(i, (i + shift) % size) for i in range(size)])  17.9 us
    pallas_call x8, Pallas kernels, call(): pl.pallas_call(kernel, out_shape=[shaped(*out) for out in outs], in_specs...  14.4 us
    all_to_all x1, blocking collectives, step(): partial_router = lax.all_to_all(partial_router, NEAR, 0, 0, tiled=True)  10.5 us
    ppermute x6, waiting for transfers between devices, ring_parts(): lax.ppermute(array, axis, [(i, (i + shift) % size) for i in range(size)])  7.29 us
    all_gather x1, waiting for transfers between devices, step(): everyone = lax.all_gather(cotangent, EXP, tiled=True)  6.97 us
  transfers between devices with their start and end apart: 10, of which 7 were waited for; matrix products, arithmetic and copies ran while one was open for 1% of the time, Pallas kernels for 7%

profile of v4, /device:TPU:5, one launch (start us, length us, event | category | flops | bytes accessed | tf_op | source)
XLA Modules:
  0.0 224.6 jit_solution(15750981318112159676)
XLA Ops:
  7.2 2.5 %shard_map.93 = bf16[64,24,256]{2,1,0:T(8,128)(2,1)} custom-call(bf16[192,192]{1,0:T(8,128)(2,1)} %constant.2.clone.perm_ref, bf16[2,768,256]{2,1,0:T(8,128)(2,1)} %in_ref.1), custom_call_target="tpu_custom_call" | custom-call | tf_op jit(solution)/shard_map/pallas_call | solution.py:59
  9.6 29.6 %all-to-all-start = ((bf16[64,24,256]{2,1,0:T(8,128)(2,1)}), bf16[64,24,256]{2,1,0:T(8,128)(2,1)S(1)}, u32[]{:S(2)}, u32[]{:S(2)}) async-start(bf16[64,24,256]{2,1,0:T(8,128)(2,1)} %shard_map.93), calls=%async_computation | async-start | bytes 1572864 | tf_op jit(solution)/shard_map/all_to_all | solution.py:312
  39.2 0.0 all-gather.2.cloned.1.call-start
  39.3 0.7 all-gather.2.cloned.1.call-update
  40.0 1.2 fusion
  41.1 2.2 collective-permute-start.2
  43.3 4.4 %collective-permute-start.1 = (f32[128,128]{1,0:T(8,128)S(1)}, f32[128,128]{1,0:T(8,128)S(1)}, u32[]{:S(2)}, u32[]{:S(2)}) collective-permute-start(f32[128,128]{1,0:T(8,128)S(1)} %fusion), channel_id=1, source_target_pairs={{0,128},{64,192},{128,0},{192,64},{1,129},{65,193},{129,1},{193,65... | collective-permute-start | bytes 196616 | tf_op jit(solution)/shard_map/ppermute | solution.py:29
  47.7 1.9 collective-permute-start
  49.6 0.5 collective-permute-done.1
  50.1 2.9 %collective-permute-done = f32[128,128]{1,0:T(8,128)S(1)} collective-permute-done((f32[128,128]{1,0:T(8,128)S(1)}, f32[128,128]{1,0:T(8,128)S(1)}, u32[]{:S(2)}, u32[]{:S(2)}) %collective-permute-start) | collective-permute-done | bytes 65568 | tf_op jit(solution)/shard_map/ppermute | solution.py:29
  53.0 4.6 %collective-permute-start.5 = (f32[128,128]{1,0:T(8,128)S(1)}, f32[128,128]{1,0:T(8,128)S(1)}, u32[]{:S(2)}, u32[]{:S(2)}) collective-permute-start(f32[128,128]{1,0:T(8,128)S(1)} %add_add_fusion.1), channel_id=1, source_target_pairs={{0,768},{256,0},{512,256},{768,512},{1,769},{257,1},{513,257},{769... | collective-permute-start | bytes 196616 | tf_op jit(solution)/shard_map/ppermute | solution.py:29
  57.7 2.3 %collective-permute-start.4 = (f32[128,128]{1,0:T(8,128)S(1)}, f32[128,128]{1,0:T(8,128)S(1)}, u32[]{:S(2)}, u32[]{:S(2)}) collective-permute-start(f32[128,128]{1,0:T(8,128)S(1)} %add_add_fusion.1), channel_id=1, source_target_pairs={{0,512},{256,768},{512,0},{768,256},{1,513},{257,769},{513,1},{769... | collective-permute-start | bytes 196616 | tf_op jit(solution)/shard_map/ppermute | solution.py:29
  59.9 2.6 %collective-permute-start.3 = (f32[128,128]{1,0:T(8,128)S(1)}, f32[128,128]{1,0:T(8,128)S(1)}, u32[]{:S(2)}, u32[]{:S(2)}) collective-permute-start(f32[128,128]{1,0:T(8,128)S(1)} %add_add_fusion.1), channel_id=1, source_target_pairs={{0,256},{256,512},{512,768},{768,0},{1,257},{257,513},{513,769},{7... | collective-permute-start | bytes 196616 | tf_op jit(solution)/shard_map/ppermute | solution.py:29
  62.5 1.9 collective-permute-done.4
  64.5 2.0 collective-permute-done.3
  66.5 0.6 add_add_fusion.logits_ref
  67.1 3.7 %shard_map.94 = (f32[128,128]{1,0:T(8,128)S(1)}, f32[24,128]{1,0:T(8,128)S(1)}, f32[8,128]{1,0:T(8,128)S(1)}, bf16[3,128,1536]{2,1,0:T(8,128)(2,1)}, f32[8,8,128]{2,1,0:T(8,128)S(1)}) custom-call(f32[128,128]{1,0:T(8,128)} %add_add_fusion.logits_ref, s32[8,128]{1,0:T(8,128)} %bitcast.7), custom_call_target="tpu_custom_call" | custom-call | tf_op jit(solution)/shard_map/pallas_call | solution.py:59
  70.8 58.0 %all-to-all-done.rows_ref = bf16[64,24,256]{2,1,0:T(8,128)(2,1)S(1)} async-done(((bf16[64,24,256]{2,1,0:T(8,128)(2,1)}), bf16[64,24,256]{2,1,0:T(8,128)(2,1)S(1)}, u32[]{:S(2)}, u32[]{:S(2)}) %all-to-all-start) | async-done | bytes 786464 | tf_op jit(solution)/shard_map/all_to_all | solution.py:312
  128.8 2.3 %shard_map.96 = f32[16,8,128]{2,1,0:T(8,128)} custom-call(bf16[64,24,256]{2,1,0:T(8,128)(2,1)S(1)} %all-to-all-done.rows_ref, bf16[128,256]{1,0:T(8,128)(2,1)} %cot_ref.1, f32[8,128]{1,0:T(8,128)S(1)} %get-tuple-element.12.row_ref), custom_call_target="tpu_custom_call" | custom-call | tf_op jit(solution)/shard_map/pallas_call | solution.py:59
  131.1 6.9 %all-to-all-start.1 = ((f32[16,8,128]{2,1,0:T(8,128)}), f32[16,8,128]{2,1,0:T(8,128)S(1)}, u32[]{:S(2)}, u32[]{:S(2)}) async-start(f32[16,8,128]{2,1,0:T(8,128)} %shard_map.96), calls=%async_computation.1 | async-start | bytes 131072 | tf_op jit(solution)/shard_map/all_to_all | solution.py:338
  138.0 0.1 copy.10
  138.1 4.5 %all-to-all-done.1.parts_ref = f32[16,8,128]{2,1,0:T(8,128)S(1)} async-done(((f32[16,8,128]{2,1,0:T(8,128)}), f32[16,8,128]{2,1,0:T(8,128)S(1)}, u32[]{:S(2)}, u32[]{:S(2)}) %all-to-all-start.1) | async-done | bytes 65568 | tf_op jit(solution)/shard_map/all_to_all | solution.py:338
  142.7 1.0 shard_map.97
  143.7 10.5 %all_to_all.25.in_ref = f32[8,40,128]{2,1,0:T(8,128)S(1)} all-to-all(f32[8,40,128]{2,1,0:T(8,128)S(1)} %get-tuple-element.17), channel_id=1, replica_groups=mesh['ctx_0'=4,'ctx_1'=4,'z_hi'=8,'z_lo'=4,'core'=2] {'z_lo','core'}, dimensions={0} | all-to-all | bytes 327680 | tf_op jit(solution)/shard_map/all_to_all | solution.py:346
  154.2 39.5 %all_to_all.26.in_ref.slots_ref = f32[8,40,128]{2,1,0:T(8,128)S(1)} all-to-all(f32[8,40,128]{2,1,0:T(8,128)S(1)} %shard_map.99), channel_id=1, replica_groups=mesh['ctx_0'=4,'ctx_1'=4,'z_hi'=8,'z_lo'=4,'core'=2] {'z_hi'}, dimensions={0} | all-to-all | bytes 327680 | tf_op jit(solution)/shard_map/all_to_all | solution.py:348
  193.7 0.7 shard_map.100
  194.4 6.9 %all-to-all-start.4 = ((f32[8,32,128]{2,1,0:T(8,128)}), f32[8,32,128]{2,1,0:T(8,128)S(1)}, u32[]{:S(2)}, u32[]{:S(2)}) async-start(f32[8,32,128]{2,1,0:T(8,128)} %shard_map.100), calls=%async_computation.4 | async-start | bytes 262144 | tf_op jit(solution)/shard_map/all_to_all | solution.py:350
  201.3 2.4 %shard_map.95 = bf16[128,256]{1,0:T(8,128)(2,1)} custom-call(bf16[64,24,256]{2,1,0:T(8,128)(2,1)S(1)} %all-to-all-done.rows_ref, bf16[3,128,1536]{2,1,0:T(8,128)(2,1)} %get-tuple-element.11.wt_ref), custom_call_target="tpu_custom_call" | custom-call | tf_op jit(solution)/shard_map/pallas_call | solution.py:59
  203.7 1.9 shard_map.98
  205.5 7.0 %all-gather.2.cloned.1.call-done.all_ref = bf16[8192,256]{1,0:T(8,128)(2,1)} async-done(((bf16[128,256]{1,0:T(8,128)(2,1)}), bf16[8192,256]{1,0:T(8,128)(2,1)}) %all-gather.2.cloned.1.call-update) | async-done | bytes 4194320 | tf_op jit(solution)/shard_map/all_gather | solution.py:310
  212.5 4.6 %shard_map.101 = bf16[2,768,256]{2,1,0:T(8,128)(2,1)} custom-call(f32[8,40,128]{2,1,0:T(8,128)S(1)} %all_to_all.26.in_ref.slots_ref, bf16[8192,256]{1,0:T(8,128)(2,1)} %all-gather.2.cloned.1.call-done.all_ref), custom_call_target="tpu_custom_call" | custom-call | tf_op jit(solution)/shard_map/pallas_call | solution.py:285
  217.1 0.7 copy.12
  (7 shorter events, 0.1 us)
Async XLA Ops:
  7.2 130.9 %copy-start = (bf16[128,256]{1,0:T(8,128)(2,1)S(1)}, bf16[128,256]{1,0:T(8,128)(2,1)}, u32[]{:S(2)}) copy-start(bf16[128,256]{1,0:T(8,128)(2,1)} %param.6) | copy-start | bytes 196612
  9.6 119.2 %all-to-all-start = ((bf16[64,24,256]{2,1,0:T(8,128)(2,1)}), bf16[64,24,256]{2,1,0:T(8,128)(2,1)S(1)}, u32[]{:S(2)}, u32[]{:S(2)}) async-start(bf16[64,24,256]{2,1,0:T(8,128)(2,1)} %shard_map.93), calls=%async_computation | async-start | bytes 1572864 | tf_op jit(solution)/shard_map/all_to_all | solution.py:312
  39.2 173.3 %all-gather.2.cloned.1.call-start = ((), (), s32[]{:S(2)}) async-start(), calls=%async_computation.5 | async-start | bytes 4259840 | tf_op jit(solution)/shard_map/all_gather | solution.py:310
  41.1 8.5 %collective-permute-start.2 = (f32[128,128]{1,0:T(8,128)S(1)}, f32[128,128]{1,0:T(8,128)S(1)}, u32[]{:S(2)}, u32[]{:S(2)}) collective-permute-start(f32[128,128]{1,0:T(8,128)S(1)} %fusion), channel_id=1, source_target_pairs={{0,192},{64,0},{128,64},{192,128},{1,193},{65,1},{129,65},{193,129... | collective-permute-start | bytes 196616 | tf_op jit(solution)/shard_map/ppermute | solution.py:29
  43.3 6.8 %collective-permute-start.1 = (f32[128,128]{1,0:T(8,128)S(1)}, f32[128,128]{1,0:T(8,128)S(1)}, u32[]{:S(2)}, u32[]{:S(2)}) collective-permute-start(f32[128,128]{1,0:T(8,128)S(1)} %fusion), channel_id=1, source_target_pairs={{0,128},{64,192},{128,0},{192,64},{1,129},{65,193},{129,1},{193,65... | collective-permute-start | bytes 196616 | tf_op jit(solution)/shard_map/ppermute | solution.py:29
  47.7 5.3 %collective-permute-start = (f32[128,128]{1,0:T(8,128)S(1)}, f32[128,128]{1,0:T(8,128)S(1)}, u32[]{:S(2)}, u32[]{:S(2)}) collective-permute-start(f32[128,128]{1,0:T(8,128)S(1)} %fusion), channel_id=1, source_target_pairs={{0,64},{64,128},{128,192},{192,0},{1,65},{65,129},{129,193},{193,1... | collective-permute-start | bytes 196616 | tf_op jit(solution)/shard_map/ppermute | solution.py:29
  53.0 9.5 %collective-permute-start.5 = (f32[128,128]{1,0:T(8,128)S(1)}, f32[128,128]{1,0:T(8,128)S(1)}, u32[]{:S(2)}, u32[]{:S(2)}) collective-permute-start(f32[128,128]{1,0:T(8,128)S(1)} %add_add_fusion.1), channel_id=1, source_target_pairs={{0,768},{256,0},{512,256},{768,512},{1,769},{257,1},{513,257},{769... | collective-permute-start | bytes 196616 | tf_op jit(solution)/shard_map/ppermute | solution.py:29
  57.7 6.8 %collective-permute-start.4 = (f32[128,128]{1,0:T(8,128)S(1)}, f32[128,128]{1,0:T(8,128)S(1)}, u32[]{:S(2)}, u32[]{:S(2)}) collective-permute-start(f32[128,128]{1,0:T(8,128)S(1)} %add_add_fusion.1), channel_id=1, source_target_pairs={{0,512},{256,768},{512,0},{768,256},{1,513},{257,769},{513,1},{769... | collective-permute-start | bytes 196616 | tf_op jit(solution)/shard_map/ppermute | solution.py:29
  59.9 6.5 %collective-permute-start.3 = (f32[128,128]{1,0:T(8,128)S(1)}, f32[128,128]{1,0:T(8,128)S(1)}, u32[]{:S(2)}, u32[]{:S(2)}) collective-permute-start(f32[128,128]{1,0:T(8,128)S(1)} %add_add_fusion.1), channel_id=1, source_target_pairs={{0,256},{256,512},{512,768},{768,0},{1,257},{257,513},{513,769},{7... | collective-permute-start | bytes 196616 | tf_op jit(solution)/shard_map/ppermute | solution.py:29
  131.1 11.6 %all-to-all-start.1 = ((f32[16,8,128]{2,1,0:T(8,128)}), f32[16,8,128]{2,1,0:T(8,128)S(1)}, u32[]{:S(2)}, u32[]{:S(2)}) async-start(f32[16,8,128]{2,1,0:T(8,128)} %shard_map.96), calls=%async_computation.1 | async-start | bytes 131072 | tf_op jit(solution)/shard_map/all_to_all | solution.py:338
  194.4 22.7 %all-to-all-start.4 = ((f32[8,32,128]{2,1,0:T(8,128)}), f32[8,32,128]{2,1,0:T(8,128)S(1)}, u32[]{:S(2)}, u32[]{:S(2)}) async-start(f32[8,32,128]{2,1,0:T(8,128)} %shard_map.100), calls=%async_computation.4 | async-start | bytes 262144 | tf_op jit(solution)/shard_map/all_to_all | solution.py:350
Sparse Core Ops, SparseCore 0:
  42.7 169.7 all-gather.1

commit v5 on v4

--- a/solution.py
+++ b/solution.py
@@ -11,15 +11,26 @@
 
 
 CTX = ("ctx_0", "ctx_1")
-FAR = "z_hi"
-NEAR = ("z_lo", "core")
-EXP = ("z_hi", "z_lo", "core")
-SPREAD = ("z_lo", "z_hi", "core")
+EXP = "exp"
+NEAR = 8
 F32 = jnp.float32
 BF16 = jnp.bfloat16
 INTERPRET = False
 NT = (((1,), (1,)), ((), ()))
 HIGHEST = lax.Precision.HIGHEST
+
+
+def row_order(devices):
+    chips = devices // 2
+    low, high = NEAR // 2, devices // NEAR
+    first = chips // 2 + 2
+    return [
+        (first + h * low + l) % chips * 2 + core for l in range(low) for h in range(high) for core in range(2)
+    ]
+
+
+def exchange(array, groups):
+    return lax.all_to_all(array, EXP, 0, 0, tiled=True, axis_index_groups=groups)
 
 
 def ring_parts(array, axis):
@@ -65,7 +76,7 @@
     )(*[near_memory(a) if v else a for a, v in zip(args, vmem)])
 
 
-def pack_kernel(perm_ref, in_ref, out_ref):
+def pack_kernel(places, perm_ref, in_ref, out_ref):
     local, _, width = in_ref.shape
     dests, each, _ = out_ref.shape
     span = perm_ref.shape[0] // local
@@ -75,12 +86,14 @@
         rows = jnp.concatenate([in_ref[e, c * span : (c + 1) * span, :] for e in range(local)], axis=0)
         out = jnp.dot(perm, rows, preferred_element_type=F32).astype(BF16)
         out = out.reshape(group, each, width)
-        for low in range(group // 2):
-            at = low * 2 * (dests // group) + 2 * c
-            out_ref[at : at + 2] = out[2 * low : 2 * low + 2]
-
-
-def pack_rows(expert_out, sources, capacity, group):
+        for q in range(0, group, 2):
+            at = places[c * group + q]
+            out_ref[at : at + 2] = out[q : q + 2]
+
+
+def pack_rows(expert_out, order, capacity, group):
+    sources = len(order)
+    places = [order.index(s) for s in range(sources)]
     local, _, width = expert_out.shape
     span = group * capacity
     perm = np.zeros((local * span, local * span), np.float32)
@@ -89,13 +102,13 @@
             for c in range(capacity):
                 perm[(s * local + e) * capacity + c, e * span + s * capacity + c] = 1.0
     return call(
-        pack_kernel,
+        functools.partial(pack_kernel, places),
         [((sources, local * capacity, width), BF16, True)],
         jnp.asarray(perm, BF16), expert_out,
     )[0]
 
 
-def gate_kernel(capacity, logits_ref, routes_ref, probs_ref, small_ref, row_ref, wt_ref, slots_ref):
+def gate_kernel(capacity, first, logits_ref, routes_ref, probs_ref, small_ref, row_ref, wt_ref, slots_ref):
     logits = logits_ref[...]
     experts, tokens = logits.shape
     top = routes_ref.shape[0]
@@ -122,9 +135,10 @@
     upper = jnp.where(before < after, 1.0, 0.0).astype(BF16)
     position = jnp.dot(member.astype(BF16), upper, preferred_element_type=F32)
     near, far, _ = slots_ref.shape
-    span = experts // far
-    high, rest = which // span, which % span
-    order = (rest // 4) * (4 * far) + high * 4 + rest % 4
+    chips = experts // 4
+    chip = (which // 4 + chips - first) % chips
+    low = near // 2
+    order = (chip % low) * (4 * far) + chip // low * 4 + which % 4
     place = order.astype(F32) * float(capacity) + position
     row = jnp.concatenate(
         [jnp.sum(jnp.where(hit, place, 0.0), axis=0, keepdims=True) for hit in hits], axis=0
@@ -299,8 +313,11 @@
     rows, top = routes.shape
     local = expert_out.shape[0]
     sources = lax.axis_size(EXP)
-    near = lax.axis_size(NEAR)
-    far = lax.axis_size(FAR)
+    near = NEAR
+    far = sources // near
+    order = row_order(sources)
+    near_groups = [[f * near + n for n in range(near)] for f in range(far)]
+    far_groups = [[f * near + n for f in range(far)] for n in range(near)]
     experts = local * sources
     capacity = expert_out.shape[1] // sources
     width = tokens.shape[1]
@@ -308,8 +325,8 @@
     routes_t = routes.T
 
     everyone = lax.all_gather(cotangent, EXP, tiled=True)
-    sent = pack_rows(expert_out, sources, capacity, near)
-    arrived = lax.all_to_all(sent, SPREAD, 0, 0, tiled=True)
+    sent = pack_rows(expert_out, order, capacity, near)
+    arrived = exchange(sent, [order])
 
     partial_logits = lax.dot_general(
         router_weight, tokens.astype(F32), (((0,), (1,)), ((), ())), precision=HIGHEST
@@ -318,7 +335,7 @@
     logits = ring_sum(logits, CTX[0])
     square = (experts, rows)
     probs, small, row, wt, slots = call(
-        functools.partial(gate_kernel, capacity),
+        functools.partial(gate_kernel, capacity, order[0] // 2),
         [
             (square, F32, True),
             ((3 * top, rows), F32, True),
@@ -336,18 +353,20 @@
         vmem=(True, False, True),
     )[0]
     dots = lax.all_to_all(partial_dots, CTX, 0, 0, tiled=True)
-    mixed = call(mixed_kernel, [((rows, width), BF16, False)], arrived, wt, vmem=(True, False))[0]
+    mixed = call(
+        mixed_kernel, [((rows, width), BF16, False)], arrived, wt, vmem=(True, False)
+    )[0]
     partial_router, dlog = call(
         router_kernel,
         [((near, share + far, experts), F32, True), (square, F32, True)],
         dots, routes_t, small, probs, tokens.T, slots,
         vmem=(True, False, True, True, True, True),
     )
-    partial_router = lax.all_to_all(partial_router, NEAR, 0, 0, tiled=True)
+    partial_router = exchange(partial_router, near_groups)
     mine = call(near_kernel, [((far, share + near, experts), F32, True)], partial_router, vmem=(True,))[0]
-    mine = lax.all_to_all(mine, FAR, 0, 0, tiled=True)
+    mine = exchange(mine, far_groups)
     total = call(far_kernel, [((near, share, experts), F32, True)], mine, vmem=(True,))[0]
-    router_grad = lax.all_to_all(total, NEAR, 0, 0, tiled=True).reshape(width, experts)
+    router_grad = exchange(total, near_groups).reshape(width, experts)
     token_grad = call(
         token_grad_kernel, [((rows, width), BF16, False)], dlog, router_weight, vmem=(True, False)
     )[0]
@@ -358,8 +377,7 @@
 def solution(mesh):
     n = mesh.shape["exp"]
     side = 4 if mesh.shape["ctx"] == 16 else 2
-    low = 4 if n == 64 else 2
-    split = Mesh(mesh.devices.reshape(side, -1, n // (2 * low), low, 2), CTX + EXP)
+    split = Mesh(mesh.devices.reshape(side, -1, n), CTX + (EXP,))
     in_specs = (P(EXP, CTX), P(EXP, CTX), P(EXP, None), P(CTX, None), P(EXP, None, CTX))
     out_specs = (P(EXP, CTX), P(EXP, CTX), P(CTX, None), P(EXP, None, CTX))
     return jax.shard_map(step, mesh=split, in_specs=in_specs, out_specs=out_specs, check_vma=False)

time: 226 us -> 221 us (0.978)
  the two profiles are of different devices: /device:TPU:5 before, /device:TPU:1 now
where the time goes in v5:
time: 221 us; the launch traced here: 220 us
  starting transfers between devices  67.9 us (31%)
  waiting for transfers between devices  58.4 us (26%)
  blocking collectives  58.3 us (26%)
  Pallas kernels  19 us (9%)
  between operations  14.2 us (6%)
    all_to_all x2, blocking collectives, exchange(): lax.all_to_all(array, EXP, 0, 0, tiled=True, axis_index_groups=groups)  58.3 us
    all_to_all x2, waiting for transfers between devices, exchange(): lax.all_to_all(array, EXP, 0, 0, tiled=True, axis_index_groups=groups)  43.2 us
    all_to_all x2, starting transfers between devices, exchange(): lax.all_to_all(array, EXP, 0, 0, tiled=True, axis_index_groups=groups)  42.3 us
    ppermute x6, starting transfers between devices, ring_parts(): lax.ppermute(array, axis, [(i, (i + shift) % size) for i in range(size)])  18.8 us
    pallas_call x8, Pallas kernels, call(): pl.pallas_call(kernel, out_shape=[shaped(*out) for out in outs], in_specs...  14.4 us
    ppermute x6, waiting for transfers between devices, ring_parts(): lax.ppermute(array, axis, [(i, (i + shift) % size) for i in range(size)])  8.08 us
    all_to_all x1, starting transfers between devices, step(): dots = lax.all_to_all(partial_dots, CTX, 0, 0, tiled=True)  6.71 us
    all_to_all x1, waiting for transfers between devices, step(): dots = lax.all_to_all(partial_dots, CTX, 0, 0, tiled=True)  6.39 us
  transfers between devices with their start and end apart: 10, of which 6 were waited for; matrix products, arithmetic and copies ran while one was open for 1% of the time, Pallas kernels for 7%

profile of v5, /device:TPU:1, one launch (start us, length us, event | category | flops | bytes accessed | tf_op | source)
XLA Modules:
  0.0 220.4 jit_solution(10299673409857717500)
XLA Ops:
  7.2 0.0 copy-start
  7.2 2.5 %shard_map.93 = bf16[64,24,256]{2,1,0:T(8,128)(2,1)} custom-call(bf16[192,192]{1,0:T(8,128)(2,1)} %constant.2.clone.perm_ref, bf16[2,768,256]{2,1,0:T(8,128)(2,1)} %in_ref.1), custom_call_target="tpu_custom_call" | custom-call | tf_op jit(solution)/shard_map/pallas_call | solution.py:70
  9.6 35.7 %all-to-all-start = ((bf16[64,24,256]{2,1,0:T(8,128)(2,1)}), bf16[64,24,256]{2,1,0:T(8,128)(2,1)S(1)}, u32[]{:S(2)}, u32[]{:S(2)}) async-start(bf16[64,24,256]{2,1,0:T(8,128)(2,1)} %shard_map.93), calls=%async_computation | async-start | bytes 1572864 | tf_op jit(solution)/shard_map/all_to_all | solution.py:33
  45.4 0.0 all-gather.2.cloned.1.call-start
  45.4 0.7 all-gather.2.cloned.1.call-update
  46.1 1.2 fusion
  47.3 4.4 %collective-permute-start.2 = (f32[128,128]{1,0:T(8,128)S(1)}, f32[128,128]{1,0:T(8,128)S(1)}, u32[]{:S(2)}, u32[]{:S(2)}) collective-permute-start(f32[128,128]{1,0:T(8,128)S(1)} %fusion), channel_id=1, source_target_pairs={{0,192},{64,0},{128,64},{192,128},{1,193},{65,1},{129,65},{193,129... | collective-permute-start | bytes 196616 | tf_op jit(solution)/shard_map/ppermute | solution.py:40
  51.7 2.4 %collective-permute-start.1 = (f32[128,128]{1,0:T(8,128)S(1)}, f32[128,128]{1,0:T(8,128)S(1)}, u32[]{:S(2)}, u32[]{:S(2)}) collective-permute-start(f32[128,128]{1,0:T(8,128)S(1)} %fusion), channel_id=1, source_target_pairs={{0,128},{64,192},{128,0},{192,64},{1,129},{65,193},{129,1},{193,65... | collective-permute-start | bytes 196616 | tf_op jit(solution)/shard_map/ppermute | solution.py:40
  54.1 2.5 %collective-permute-start = (f32[128,128]{1,0:T(8,128)S(1)}, f32[128,128]{1,0:T(8,128)S(1)}, u32[]{:S(2)}, u32[]{:S(2)}) collective-permute-start(f32[128,128]{1,0:T(8,128)S(1)} %fusion), channel_id=1, source_target_pairs={{0,64},{64,128},{128,192},{192,0},{1,65},{65,129},{129,193},{193,1... | collective-permute-start | bytes 196616 | tf_op jit(solution)/shard_map/ppermute | solution.py:40
  56.7 1.8 collective-permute-done.1
  58.5 2.1 collective-permute-done
  60.7 4.6 %collective-permute-start.5 = (f32[128,128]{1,0:T(8,128)S(1)}, f32[128,128]{1,0:T(8,128)S(1)}, u32[]{:S(2)}, u32[]{:S(2)}) collective-permute-start(f32[128,128]{1,0:T(8,128)S(1)} %add_add_fusion.1), channel_id=1, source_target_pairs={{0,768},{256,0},{512,256},{768,512},{1,769},{257,1},{513,257},{769... | collective-permute-start | bytes 196616 | tf_op jit(solution)/shard_map/ppermute | solution.py:40
  65.3 2.3 %collective-permute-start.4 = (f32[128,128]{1,0:T(8,128)S(1)}, f32[128,128]{1,0:T(8,128)S(1)}, u32[]{:S(2)}, u32[]{:S(2)}) collective-permute-start(f32[128,128]{1,0:T(8,128)S(1)} %add_add_fusion.1), channel_id=1, source_target_pairs={{0,512},{256,768},{512,0},{768,256},{1,513},{257,769},{513,1},{769... | collective-permute-start | bytes 196616 | tf_op jit(solution)/shard_map/ppermute | solution.py:40
  67.6 2.6 %collective-permute-start.3 = (f32[128,128]{1,0:T(8,128)S(1)}, f32[128,128]{1,0:T(8,128)S(1)}, u32[]{:S(2)}, u32[]{:S(2)}) collective-permute-start(f32[128,128]{1,0:T(8,128)S(1)} %add_add_fusion.1), channel_id=1, source_target_pairs={{0,256},{256,512},{512,768},{768,0},{1,257},{257,513},{513,769},{7... | collective-permute-start | bytes 196616 | tf_op jit(solution)/shard_map/ppermute | solution.py:40
  70.2 1.9 collective-permute-done.4
  72.1 2.2 collective-permute-done.3
  74.3 0.6 add_add_fusion.logits_ref
  75.0 3.7 %shard_map.94 = (f32[128,128]{1,0:T(8,128)S(1)}, f32[24,128]{1,0:T(8,128)S(1)}, f32[8,128]{1,0:T(8,128)S(1)}, bf16[3,128,1536]{2,1,0:T(8,128)(2,1)}, f32[8,8,128]{2,1,0:T(8,128)S(1)}) custom-call(f32[128,128]{1,0:T(8,128)} %add_add_fusion.logits_ref, s32[8,128]{1,0:T(8,128)} %bitcast.7), custom_call_target="tpu_custom_call" | custom-call | tf_op jit(solution)/shard_map/pallas_call | solution.py:70
  78.7 43.2 %all-to-all-done.rows_ref = bf16[64,24,256]{2,1,0:T(8,128)(2,1)S(1)} async-done(((bf16[64,24,256]{2,1,0:T(8,128)(2,1)}), bf16[64,24,256]{2,1,0:T(8,128)(2,1)S(1)}, u32[]{:S(2)}, u32[]{:S(2)}) %all-to-all-start) | async-done | bytes 786464 | tf_op jit(solution)/shard_map/all_to_all | solution.py:33
  121.9 2.3 %shard_map.96 = f32[16,8,128]{2,1,0:T(8,128)} custom-call(bf16[64,24,256]{2,1,0:T(8,128)(2,1)S(1)} %all-to-all-done.rows_ref, bf16[128,256]{1,0:T(8,128)(2,1)} %cot_ref.1, f32[8,128]{1,0:T(8,128)S(1)} %get-tuple-element.12.row_ref), custom_call_target="tpu_custom_call" | custom-call | tf_op jit(solution)/shard_map/pallas_call | solution.py:70
  124.2 6.7 %all-to-all-start.1 = ((f32[16,8,128]{2,1,0:T(8,128)}), f32[16,8,128]{2,1,0:T(8,128)S(1)}, u32[]{:S(2)}, u32[]{:S(2)}) async-start(f32[16,8,128]{2,1,0:T(8,128)} %shard_map.96), calls=%async_computation.1 | async-start | bytes 131072 | tf_op jit(solution)/shard_map/all_to_all | solution.py:355
  130.9 0.1 copy.10
  131.0 6.4 %all-to-all-done.1.parts_ref = f32[16,8,128]{2,1,0:T(8,128)S(1)} async-done(((f32[16,8,128]{2,1,0:T(8,128)}), f32[16,8,128]{2,1,0:T(8,128)S(1)}, u32[]{:S(2)}, u32[]{:S(2)}) %all-to-all-start.1) | async-done | bytes 65568 | tf_op jit(solution)/shard_map/all_to_all | solution.py:355
  137.4 1.0 shard_map.97
  138.4 10.1 %all_to_all.25.in_ref = f32[8,40,128]{2,1,0:T(8,128)S(1)} all-to-all(f32[8,40,128]{2,1,0:T(8,128)S(1)} %get-tuple-element.17), channel_id=1, replica_groups={{0,1,2,3,4,5,6,7},{8,9,10,11,12,13,14,15},{16,17,18,19,20,21,22,23},{24..., dimensions={0} | all-to-all | bytes 327680 | tf_op jit(solution)/shard_map/all_to_all | solution.py:33
  148.5 48.3 %all_to_all.26.in_ref.slots_ref = f32[8,40,128]{2,1,0:T(8,128)S(1)} all-to-all(f32[8,40,128]{2,1,0:T(8,128)S(1)} %shard_map.99), channel_id=1, replica_groups={{0,8,16,24,32,40,48,56},{1,9,17,25,33,41,49,57},{2,10,18,26,34,42,50,58..., dimensions={0} | all-to-all | bytes 327680 | tf_op jit(solution)/shard_map/all_to_all | solution.py:33
  196.8 0.7 shard_map.100
  197.4 6.6 %all-to-all-start.4 = ((f32[8,32,128]{2,1,0:T(8,128)}), f32[8,32,128]{2,1,0:T(8,128)S(1)}, u32[]{:S(2)}, u32[]{:S(2)}) async-start(f32[8,32,128]{2,1,0:T(8,128)} %shard_map.100), calls=%async_computation.4 | async-start | bytes 262144 | tf_op jit(solution)/shard_map/all_to_all | solution.py:33
  204.1 2.4 %shard_map.95 = bf16[128,256]{1,0:T(8,128)(2,1)} custom-call(bf16[64,24,256]{2,1,0:T(8,128)(2,1)S(1)} %all-to-all-done.rows_ref, bf16[3,128,1536]{2,1,0:T(8,128)(2,1)} %get-tuple-element.11.wt_ref), custom_call_target="tpu_custom_call" | custom-call | tf_op jit(solution)/shard_map/pallas_call | solution.py:70
  206.4 1.9 shard_map.98
  208.3 4.6 %shard_map.101 = bf16[2,768,256]{2,1,0:T(8,128)(2,1)} custom-call(f32[8,40,128]{2,1,0:T(8,128)S(1)} %all_to_all.26.in_ref.slots_ref, bf16[8192,256]{1,0:T(8,128)(2,1)} %all-gather.2.cloned.1.call-done.all_ref), custom_call_target="tpu_custom_call" | custom-call | tf_op jit(solution)/shard_map/pallas_call | solution.py:299
  212.9 0.7 copy.12
  (7 shorter events, 0.1 us)
Async XLA Ops:
  7.2 123.7 %copy-start = (bf16[128,256]{1,0:T(8,128)(2,1)S(1)}, bf16[128,256]{1,0:T(8,128)(2,1)}, u32[]{:S(2)}) copy-start(bf16[128,256]{1,0:T(8,128)(2,1)} %param.6) | copy-start | bytes 196612
  9.6 112.3 %all-to-all-start = ((bf16[64,24,256]{2,1,0:T(8,128)(2,1)}), bf16[64,24,256]{2,1,0:T(8,128)(2,1)S(1)}, u32[]{:S(2)}, u32[]{:S(2)}) async-start(bf16[64,24,256]{2,1,0:T(8,128)(2,1)} %shard_map.93), calls=%async_computation | async-start | bytes 1572864 | tf_op jit(solution)/shard_map/all_to_all | solution.py:33
  45.4 162.9 %all-gather.2.cloned.1.call-start = ((), (), s32[]{:S(2)}) async-start(), calls=%async_computation.5 | async-start | bytes 4259840 | tf_op jit(solution)/shard_map/all_gather | solution.py:327
  47.3 9.4 %collective-permute-start.2 = (f32[128,128]{1,0:T(8,128)S(1)}, f32[128,128]{1,0:T(8,128)S(1)}, u32[]{:S(2)}, u32[]{:S(2)}) collective-permute-start(f32[128,128]{1,0:T(8,128)S(1)} %fusion), channel_id=1, source_target_pairs={{0,192},{64,0},{128,64},{192,128},{1,193},{65,1},{129,65},{193,129... | collective-permute-start | bytes 196616 | tf_op jit(solution)/shard_map/ppermute | solution.py:40
  51.7 6.8 %collective-permute-start.1 = (f32[128,128]{1,0:T(8,128)S(1)}, f32[128,128]{1,0:T(8,128)S(1)}, u32[]{:S(2)}, u32[]{:S(2)}) collective-permute-start(f32[128,128]{1,0:T(8,128)S(1)} %fusion), channel_id=1, source_target_pairs={{0,128},{64,192},{128,0},{192,64},{1,129},{65,193},{129,1},{193,65... | collective-permute-start | bytes 196616 | tf_op jit(solution)/shard_map/ppermute | solution.py:40
  54.1 6.5 %collective-permute-start = (f32[128,128]{1,0:T(8,128)S(1)}, f32[128,128]{1,0:T(8,128)S(1)}, u32[]{:S(2)}, u32[]{:S(2)}) collective-permute-start(f32[128,128]{1,0:T(8,128)S(1)} %fusion), channel_id=1, source_target_pairs={{0,64},{64,128},{128,192},{192,0},{1,65},{65,129},{129,193},{193,1... | collective-permute-start | bytes 196616 | tf_op jit(solution)/shard_map/ppermute | solution.py:40
  60.7 9.5 %collective-permute-start.5 = (f32[128,128]{1,0:T(8,128)S(1)}, f32[128,128]{1,0:T(8,128)S(1)}, u32[]{:S(2)}, u32[]{:S(2)}) collective-permute-start(f32[128,128]{1,0:T(8,128)S(1)} %add_add_fusion.1), channel_id=1, source_target_pairs={{0,768},{256,0},{512,256},{768,512},{1,769},{257,1},{513,257},{769... | collective-permute-start | bytes 196616 | tf_op jit(solution)/shard_map/ppermute | solution.py:40
  65.3 6.8 %collective-permute-start.4 = (f32[128,128]{1,0:T(8,128)S(1)}, f32[128,128]{1,0:T(8,128)S(1)}, u32[]{:S(2)}, u32[]{:S(2)}) collective-permute-start(f32[128,128]{1,0:T(8,128)S(1)} %add_add_fusion.1), channel_id=1, source_target_pairs={{0,512},{256,768},{512,0},{768,256},{1,513},{257,769},{513,1},{769... | collective-permute-start | bytes 196616 | tf_op jit(solution)/shard_map/ppermute | solution.py:40
  67.6 6.7 %collective-permute-start.3 = (f32[128,128]{1,0:T(8,128)S(1)}, f32[128,128]{1,0:T(8,128)S(1)}, u32[]{:S(2)}, u32[]{:S(2)}) collective-permute-start(f32[128,128]{1,0:T(8,128)S(1)} %add_add_fusion.1), channel_id=1, source_target_pairs={{0,256},{256,512},{512,768},{768,0},{1,257},{257,513},{513,769},{7... | collective-permute-start | bytes 196616 | tf_op jit(solution)/shard_map/ppermute | solution.py:40
  124.2 13.2 %all-to-all-start.1 = ((f32[16,8,128]{2,1,0:T(8,128)}), f32[16,8,128]{2,1,0:T(8,128)S(1)}, u32[]{:S(2)}, u32[]{:S(2)}) async-start(f32[16,8,128]{2,1,0:T(8,128)} %shard_map.96), calls=%async_computation.1 | async-start | bytes 131072 | tf_op jit(solution)/shard_map/all_to_all | solution.py:355
  197.4 15.5 %all-to-all-start.4 = ((f32[8,32,128]{2,1,0:T(8,128)}), f32[8,32,128]{2,1,0:T(8,128)S(1)}, u32[]{:S(2)}, u32[]{:S(2)}) async-start(f32[8,32,128]{2,1,0:T(8,128)} %shard_map.100), calls=%async_computation.4 | async-start | bytes 262144 | tf_op jit(solution)/shard_map/all_to_all | solution.py:33
Sparse Core Ops, SparseCore 0:
  48.9 154.2 all-gather.1

commit v6 on v5

--- a/solution.py
+++ b/solution.py
@@ -240,8 +240,9 @@
         total = total + in_ref[n, 0:share, :]
     for f in range(far):
         out_ref[f, 0:share, :] = total
+        dest = (f + far // 2) % far
         for n in range(near):
-            out_ref[f, share + n : share + n + 1, :] = in_ref[n, share + f : share + f + 1, :]
+            out_ref[f, share + n : share + n + 1, :] = in_ref[n, share + dest : share + dest + 1, :]
 
 
 def far_kernel(in_ref, out_ref):
@@ -262,6 +263,7 @@
 
 def owner_kernel(capacity, near, tokens, pair, slots_ref, all_ref, out_ref):
     local = out_ref.shape[0]
+    far = slots_ref.shape[0]
     share = slots_ref.shape[1] - near
     group = 4
     rows = group * capacity
@@ -272,7 +274,7 @@
     column = lax.broadcasted_iota(jnp.int32, (rows, group * tokens), 1).astype(F32)
     base = (source[:, 0:1] * tokens).astype(F32)
     for h in range(pair * near // group):
-        step = pl.program_id(0) * pair + h * group // near
+        step = (pl.program_id(0) * pair + h * group // near + far // 2) % far
         at = share + h * group % near
         table = jnp.broadcast_to(slots_ref[step, at : at + 1, :], (rows, 128))
         for q in range(1, group):
@@ -317,7 +319,8 @@
     far = sources // near
     order = row_order(sources)
     near_groups = [[f * near + n for n in range(near)] for f in range(far)]
-    far_groups = [[f * near + n for f in range(far)] for n in range(near)]
+    turn = far // 2
+    far_groups = [[(f + turn) % far * near + n for f in range(far)] for n in range(near)]
     experts = local * sources
     capacity = expert_out.shape[1] // sources
     width = tokens.shape[1]

time: 221 us -> 217 us (0.982)
  blocking collectives: 58.3 us -> 48.3 us
  waiting for transfers between devices: 58.4 us -> 66.9 us
  starting transfers between devices: 67.9 us -> 65.5 us
    all_to_all x2, blocking collectives: 58.3 us -> 48.3 us  [exchange(): lax.all_to_all(array, EXP, 0, 0, tiled=True, axis_index_groups=groups)]
    all_gather x1, waiting for transfers between devices: 0.01 us -> 8.57 us  [step(): everyone = lax.all_gather(cotangent, EXP, tiled=True)]
    all_to_all x2, starting transfers between devices: 42.3 us -> 39.9 us  [exchange(): lax.all_to_all(array, EXP, 0, 0, tiled=True, axis_index_groups=groups)]
  transfers between devices with their start and end apart: 10 -> 10, of which waited for: 6 -> 7; matrix products, arithmetic and copies ran while one was open for 1% -> 1% of each run, Pallas kernels for 7% -> 8%
where the time goes in v6:
time: 217 us
  waiting for transfers between devices  66.9 us (31%)
  starting transfers between devices  65.5 us (30%)
  blocking collectives  48.3 us (22%)
  Pallas kernels  19 us (9%)
  between operations  14.2 us (7%)
    all_to_all x2, blocking collectives, exchange(): lax.all_to_all(array, EXP, 0, 0, tiled=True, axis_index_groups=groups)  48.3 us
    all_to_all x2, waiting for transfers between devices, exchange(): lax.all_to_all(array, EXP, 0, 0, tiled=True, axis_index_groups=groups)  43.2 us
    all_to_all x2, starting transfers between devices, exchange(): lax.all_to_all(array, EXP, 0, 0, tiled=True, axis_index_groups=groups)  39.9 us
    ppermute x6, starting transfers between devices, ring_parts(): lax.ppermute(array, axis, [(i, (i + shift) % size) for i in range(size)])  18.8 us
    pallas_call x8, Pallas kernels, call(): pl.pallas_call(kernel, out_shape=[shaped(*out) for out in outs], in_specs...  14.4 us
    all_gather x1, waiting for transfers between devices, step(): everyone = lax.all_gather(cotangent, EXP, tiled=True)  8.57 us
    ppermute x6, waiting for transfers between devices, ring_parts(): lax.ppermute(array, axis, [(i, (i + shift) % size) for i in range(size)])  8.08 us
    all_to_all x1, starting transfers between devices, step(): dots = lax.all_to_all(partial_dots, CTX, 0, 0, tiled=True)  6.71 us
  transfers between devices with their start and end apart: 10, of which 7 were waited for; matrix products, arithmetic and copies ran while one was open for 1% of the time, Pallas kernels for 8%

profile of v6, /device:TPU:1, one launch (start us, length us, event | category | flops | bytes accessed | tf_op | source)
XLA Modules:
  0.0 216.5 jit_solution(5126969279562007515)
XLA Ops:
  7.2 2.5 %shard_map.93 = bf16[64,24,256]{2,1,0:T(8,128)(2,1)} custom-call(bf16[192,192]{1,0:T(8,128)(2,1)} %constant.2.clone.perm_ref, bf16[2,768,256]{2,1,0:T(8,128)(2,1)} %in_ref.1), custom_call_target="tpu_custom_call" | custom-call | tf_op jit(solution)/shard_map/pallas_call | solution.py:70
  9.6 35.7 %all-to-all-start = ((bf16[64,24,256]{2,1,0:T(8,128)(2,1)}), bf16[64,24,256]{2,1,0:T(8,128)(2,1)S(1)}, u32[]{:S(2)}, u32[]{:S(2)}) async-start(bf16[64,24,256]{2,1,0:T(8,128)(2,1)} %shard_map.93), calls=%async_computation | async-start | bytes 1572864 | tf_op jit(solution)/shard_map/all_to_all | solution.py:33
  45.4 0.0 all-gather.2.cloned.1.call-start
  45.4 0.7 all-gather.2.cloned.1.call-update
  46.1 1.2 fusion
  47.3 4.4 %collective-permute-start.2 = (f32[128,128]{1,0:T(8,128)S(1)}, f32[128,128]{1,0:T(8,128)S(1)}, u32[]{:S(2)}, u32[]{:S(2)}) collective-permute-start(f32[128,128]{1,0:T(8,128)S(1)} %fusion), channel_id=1, source_target_pairs={{0,192},{64,0},{128,64},{192,128},{1,193},{65,1},{129,65},{193,129... | collective-permute-start | bytes 196616 | tf_op jit(solution)/shard_map/ppermute | solution.py:40
  51.7 2.4 %collective-permute-start.1 = (f32[128,128]{1,0:T(8,128)S(1)}, f32[128,128]{1,0:T(8,128)S(1)}, u32[]{:S(2)}, u32[]{:S(2)}) collective-permute-start(f32[128,128]{1,0:T(8,128)S(1)} %fusion), channel_id=1, source_target_pairs={{0,128},{64,192},{128,0},{192,64},{1,129},{65,193},{129,1},{193,65... | collective-permute-start | bytes 196616 | tf_op jit(solution)/shard_map/ppermute | solution.py:40
  54.1 2.5 %collective-permute-start = (f32[128,128]{1,0:T(8,128)S(1)}, f32[128,128]{1,0:T(8,128)S(1)}, u32[]{:S(2)}, u32[]{:S(2)}) collective-permute-start(f32[128,128]{1,0:T(8,128)S(1)} %fusion), channel_id=1, source_target_pairs={{0,64},{64,128},{128,192},{192,0},{1,65},{65,129},{129,193},{193,1... | collective-permute-start | bytes 196616 | tf_op jit(solution)/shard_map/ppermute | solution.py:40
  56.7 1.8 collective-permute-done.1
  58.5 2.1 collective-permute-done
  60.7 4.6 %collective-permute-start.5 = (f32[128,128]{1,0:T(8,128)S(1)}, f32[128,128]{1,0:T(8,128)S(1)}, u32[]{:S(2)}, u32[]{:S(2)}) collective-permute-start(f32[128,128]{1,0:T(8,128)S(1)} %add_add_fusion.1), channel_id=1, source_target_pairs={{0,768},{256,0},{512,256},{768,512},{1,769},{257,1},{513,257},{769... | collective-permute-start | bytes 196616 | tf_op jit(solution)/shard_map/ppermute | solution.py:40
  65.3 2.3 %collective-permute-start.4 = (f32[128,128]{1,0:T(8,128)S(1)}, f32[128,128]{1,0:T(8,128)S(1)}, u32[]{:S(2)}, u32[]{:S(2)}) collective-permute-start(f32[128,128]{1,0:T(8,128)S(1)} %add_add_fusion.1), channel_id=1, source_target_pairs={{0,512},{256,768},{512,0},{768,256},{1,513},{257,769},{513,1},{769... | collective-permute-start | bytes 196616 | tf_op jit(solution)/shard_map/ppermute | solution.py:40
  67.6 2.6 %collective-permute-start.3 = (f32[128,128]{1,0:T(8,128)S(1)}, f32[128,128]{1,0:T(8,128)S(1)}, u32[]{:S(2)}, u32[]{:S(2)}) collective-permute-start(f32[128,128]{1,0:T(8,128)S(1)} %add_add_fusion.1), channel_id=1, source_target_pairs={{0,256},{256,512},{512,768},{768,0},{1,257},{257,513},{513,769},{7... | collective-permute-start | bytes 196616 | tf_op jit(solution)/shard_map/ppermute | solution.py:40
  70.2 1.9 collective-permute-done.4
  72.1 2.2 %collective-permute-done.3 = f32[128,128]{1,0:T(8,128)S(1)} collective-permute-done((f32[128,128]{1,0:T(8,128)S(1)}, f32[128,128]{1,0:T(8,128)S(1)}, u32[]{:S(2)}, u32[]{:S(2)}) %collective-permute-start.3) | collective-permute-done | bytes 65568 | tf_op jit(solution)/shard_map/ppermute | solution.py:40
  74.3 0.6 add_add_fusion.logits_ref
  75.0 3.7 %shard_map.94 = (f32[128,128]{1,0:T(8,128)S(1)}, f32[24,128]{1,0:T(8,128)S(1)}, f32[8,128]{1,0:T(8,128)S(1)}, bf16[3,128,1536]{2,1,0:T(8,128)(2,1)}, f32[8,8,128]{2,1,0:T(8,128)S(1)}) custom-call(f32[128,128]{1,0:T(8,128)} %add_add_fusion.logits_ref, s32[8,128]{1,0:T(8,128)} %bitcast.7), custom_call_target="tpu_custom_call" | custom-call | tf_op jit(solution)/shard_map/pallas_call | solution.py:70
  78.7 43.2 %all-to-all-done.rows_ref = bf16[64,24,256]{2,1,0:T(8,128)(2,1)S(1)} async-done(((bf16[64,24,256]{2,1,0:T(8,128)(2,1)}), bf16[64,24,256]{2,1,0:T(8,128)(2,1)S(1)}, u32[]{:S(2)}, u32[]{:S(2)}) %all-to-all-start) | async-done | bytes 786464 | tf_op jit(solution)/shard_map/all_to_all | solution.py:33
  121.9 2.3 %shard_map.96 = f32[16,8,128]{2,1,0:T(8,128)} custom-call(bf16[64,24,256]{2,1,0:T(8,128)(2,1)S(1)} %all-to-all-done.rows_ref, bf16[128,256]{1,0:T(8,128)(2,1)} %cot_ref.1, f32[8,128]{1,0:T(8,128)S(1)} %get-tuple-element.12.row_ref), custom_call_target="tpu_custom_call" | custom-call | tf_op jit(solution)/shard_map/pallas_call | solution.py:70
  124.2 6.7 %all-to-all-start.1 = ((f32[16,8,128]{2,1,0:T(8,128)}), f32[16,8,128]{2,1,0:T(8,128)S(1)}, u32[]{:S(2)}, u32[]{:S(2)}) async-start(f32[16,8,128]{2,1,0:T(8,128)} %shard_map.96), calls=%async_computation.1 | async-start | bytes 131072 | tf_op jit(solution)/shard_map/all_to_all | solution.py:358
  130.9 0.1 copy.10
  131.0 6.4 %all-to-all-done.1.parts_ref = f32[16,8,128]{2,1,0:T(8,128)S(1)} async-done(((f32[16,8,128]{2,1,0:T(8,128)}), f32[16,8,128]{2,1,0:T(8,128)S(1)}, u32[]{:S(2)}, u32[]{:S(2)}) %all-to-all-start.1) | async-done | bytes 65568 | tf_op jit(solution)/shard_map/all_to_all | solution.py:358
  137.4 1.0 shard_map.97
  138.4 10.1 %all_to_all.25.in_ref = f32[8,40,128]{2,1,0:T(8,128)S(1)} all-to-all(f32[8,40,128]{2,1,0:T(8,128)S(1)} %get-tuple-element.17), channel_id=1, replica_groups={{0,1,2,3,4,5,6,7},{8,9,10,11,12,13,14,15},{16,17,18,19,20,21,22,23},{24..., dimensions={0} | all-to-all | bytes 327680 | tf_op jit(solution)/shard_map/all_to_all | solution.py:33
  148.5 38.2 %all_to_all.26.in_ref.slots_ref = f32[8,40,128]{2,1,0:T(8,128)S(1)} all-to-all(f32[8,40,128]{2,1,0:T(8,128)S(1)} %shard_map.99), channel_id=1, replica_groups={{32,40,48,56,0,8,16,24},{33,41,49,57,1,9,17,25},{34,42,50,58,2,10,18,26..., dimensions={0} | all-to-all | bytes 327680 | tf_op jit(solution)/shard_map/all_to_all | solution.py:33
  186.7 0.7 shard_map.100
  187.4 4.2 %all-to-all-start.4 = ((f32[8,32,128]{2,1,0:T(8,128)}), f32[8,32,128]{2,1,0:T(8,128)S(1)}, u32[]{:S(2)}, u32[]{:S(2)}) async-start(f32[8,32,128]{2,1,0:T(8,128)} %shard_map.100), calls=%async_computation.4 | async-start | bytes 262144 | tf_op jit(solution)/shard_map/all_to_all | solution.py:33
  191.6 2.4 %shard_map.95 = bf16[128,256]{1,0:T(8,128)(2,1)} custom-call(bf16[64,24,256]{2,1,0:T(8,128)(2,1)S(1)} %all-to-all-done.rows_ref, bf16[3,128,1536]{2,1,0:T(8,128)(2,1)} %get-tuple-element.11.wt_ref), custom_call_target="tpu_custom_call" | custom-call | tf_op jit(solution)/shard_map/pallas_call | solution.py:70
  194.0 1.9 shard_map.98
  195.8 8.6 %all-gather.2.cloned.1.call-done.all_ref = bf16[8192,256]{1,0:T(8,128)(2,1)} async-done(((bf16[128,256]{1,0:T(8,128)(2,1)}), bf16[8192,256]{1,0:T(8,128)(2,1)}) %all-gather.2.cloned.1.call-update) | async-done | bytes 4194320 | tf_op jit(solution)/shard_map/all_gather | solution.py:330
  204.4 4.6 %shard_map.101 = bf16[2,768,256]{2,1,0:T(8,128)(2,1)} custom-call(f32[8,40,128]{2,1,0:T(8,128)S(1)} %all_to_all.26.in_ref.slots_ref, bf16[8192,256]{1,0:T(8,128)(2,1)} %all-gather.2.cloned.1.call-done.all_ref), custom_call_target="tpu_custom_call" | custom-call | tf_op jit(solution)/shard_map/pallas_call | solution.py:301
  209.0 0.7 copy.12
  (7 shorter events, 0.1 us)
Async XLA Ops:
  7.2 123.7 %copy-start = (bf16[128,256]{1,0:T(8,128)(2,1)S(1)}, bf16[128,256]{1,0:T(8,128)(2,1)}, u32[]{:S(2)}) copy-start(bf16[128,256]{1,0:T(8,128)(2,1)} %param.6) | copy-start | bytes 196612
  9.6 112.3 %all-to-all-start = ((bf16[64,24,256]{2,1,0:T(8,128)(2,1)}), bf16[64,24,256]{2,1,0:T(8,128)(2,1)S(1)}, u32[]{:S(2)}, u32[]{:S(2)}) async-start(bf16[64,24,256]{2,1,0:T(8,128)(2,1)} %shard_map.93), calls=%async_computation | async-start | bytes 1572864 | tf_op jit(solution)/shard_map/all_to_all | solution.py:33
  45.4 159.0 %all-gather.2.cloned.1.call-start = ((), (), s32[]{:S(2)}) async-start(), calls=%async_computation.5 | async-start | bytes 4259840 | tf_op jit(solution)/shard_map/all_gather | solution.py:330
  47.3 9.4 %collective-permute-start.2 = (f32[128,128]{1,0:T(8,128)S(1)}, f32[128,128]{1,0:T(8,128)S(1)}, u32[]{:S(2)}, u32[]{:S(2)}) collective-permute-start(f32[128,128]{1,0:T(8,128)S(1)} %fusion), channel_id=1, source_target_pairs={{0,192},{64,0},{128,64},{192,128},{1,193},{65,1},{129,65},{193,129... | collective-permute-start | bytes 196616 | tf_op jit(solution)/shard_map/ppermute | solution.py:40
  51.7 6.8 %collective-permute-start.1 = (f32[128,128]{1,0:T(8,128)S(1)}, f32[128,128]{1,0:T(8,128)S(1)}, u32[]{:S(2)}, u32[]{:S(2)}) collective-permute-start(f32[128,128]{1,0:T(8,128)S(1)} %fusion), channel_id=1, source_target_pairs={{0,128},{64,192},{128,0},{192,64},{1,129},{65,193},{129,1},{193,65... | collective-permute-start | bytes 196616 | tf_op jit(solution)/shard_map/ppermute | solution.py:40
  54.1 6.5 %collective-permute-start = (f32[128,128]{1,0:T(8,128)S(1)}, f32[128,128]{1,0:T(8,128)S(1)}, u32[]{:S(2)}, u32[]{:S(2)}) collective-permute-start(f32[128,128]{1,0:T(8,128)S(1)} %fusion), channel_id=1, source_target_pairs={{0,64},{64,128},{128,192},{192,0},{1,65},{65,129},{129,193},{193,1... | collective-permute-start | bytes 196616 | tf_op jit(solution)/shard_map/ppermute | solution.py:40
  60.7 9.5 %collective-permute-start.5 = (f32[128,128]{1,0:T(8,128)S(1)}, f32[128,128]{1,0:T(8,128)S(1)}, u32[]{:S(2)}, u32[]{:S(2)}) collective-permute-start(f32[128,128]{1,0:T(8,128)S(1)} %add_add_fusion.1), channel_id=1, source_target_pairs={{0,768},{256,0},{512,256},{768,512},{1,769},{257,1},{513,257},{769... | collective-permute-start | bytes 196616 | tf_op jit(solution)/shard_map/ppermute | solution.py:40
  65.3 6.8 %collective-permute-start.4 = (f32[128,128]{1,0:T(8,128)S(1)}, f32[128,128]{1,0:T(8,128)S(1)}, u32[]{:S(2)}, u32[]{:S(2)}) collective-permute-start(f32[128,128]{1,0:T(8,128)S(1)} %add_add_fusion.1), channel_id=1, source_target_pairs={{0,512},{256,768},{512,0},{768,256},{1,513},{257,769},{513,1},{769... | collective-permute-start | bytes 196616 | tf_op jit(solution)/shard_map/ppermute | solution.py:40
  67.6 6.7 %collective-permute-start.3 = (f32[128,128]{1,0:T(8,128)S(1)}, f32[128,128]{1,0:T(8,128)S(1)}, u32[]{:S(2)}, u32[]{:S(2)}) collective-permute-start(f32[128,128]{1,0:T(8,128)S(1)} %add_add_fusion.1), channel_id=1, source_target_pairs={{0,256},{256,512},{512,768},{768,0},{1,257},{257,513},{513,769},{7... | collective-permute-start | bytes 196616 | tf_op jit(solution)/shard_map/ppermute | solution.py:40
  124.2 13.2 %all-to-all-start.1 = ((f32[16,8,128]{2,1,0:T(8,128)}), f32[16,8,128]{2,1,0:T(8,128)S(1)}, u32[]{:S(2)}, u32[]{:S(2)}) async-start(f32[16,8,128]{2,1,0:T(8,128)} %shard_map.96), calls=%async_computation.1 | async-start | bytes 131072 | tf_op jit(solution)/shard_map/all_to_all | solution.py:358
  187.4 21.6 %all-to-all-start.4 = ((f32[8,32,128]{2,1,0:T(8,128)}), f32[8,32,128]{2,1,0:T(8,128)S(1)}, u32[]{:S(2)}, u32[]{:S(2)}) async-start(f32[8,32,128]{2,1,0:T(8,128)} %shard_map.100), calls=%async_computation.4 | async-start | bytes 262144 | tf_op jit(solution)/shard_map/all_to_all | solution.py:33
Sparse Core Ops, SparseCore 0:
  48.9 155.4 all-gather.1

commit v7 on v6

--- a/solution.py
+++ b/solution.py
@@ -27,6 +27,10 @@
     return [
         (first + h * low + l) % chips * 2 + core for l in range(low) for h in range(high) for core in range(2)
     ]
+
+
+def near_member(place):
+    return (place + NEAR // 2 + 1) % NEAR
 
 
 def exchange(array, groups):
@@ -166,7 +170,7 @@
         token = jnp.sum(jnp.where(here, number, 0.0), axis=1, keepdims=True)
         table = table + jnp.where(lane == s, gate, 0.0) + jnp.where(lane == 16 + s, token, 0.0)
     dest = lax.broadcasted_iota(jnp.int32, (near, far, experts), 1) * near
-    dest = dest + lax.broadcasted_iota(jnp.int32, (near, far, experts), 0)
+    dest = dest + near_member(lax.broadcasted_iota(jnp.int32, (near, far, experts), 0))
     owner = lax.broadcasted_iota(jnp.int32, (near, far, experts), 2) >> 1
     select = jnp.where(dest == owner, 1.0, 0.0).reshape(near * far, experts).astype(BF16)
     slots = sum(jnp.dot(select, term, preferred_element_type=F32) for term in split3(table))
@@ -265,6 +269,7 @@
     local = out_ref.shape[0]
     far = slots_ref.shape[0]
     share = slots_ref.shape[1] - near
+    members = [near_member(q) for q in range(near)]
     group = 4
     rows = group * capacity
     index = lax.broadcasted_iota(jnp.int32, (rows, 128), 0)
@@ -275,10 +280,10 @@
     base = (source[:, 0:1] * tokens).astype(F32)
     for h in range(pair * near // group):
         step = (pl.program_id(0) * pair + h * group // near + far // 2) % far
-        at = share + h * group % near
-        table = jnp.broadcast_to(slots_ref[step, at : at + 1, :], (rows, 128))
-        for q in range(1, group):
-            table = jnp.where(source == q, slots_ref[step, at + q : at + q + 1, :], table)
+        table = jnp.zeros((rows, 128), F32)
+        for q in range(group):
+            at = share + members.index(h * group % near + q)
+            table = jnp.where(source == q, slots_ref[step, at : at + 1, :], table)
         gates, picks = [], []
         for e in range(local):
             gates.append(jnp.sum(jnp.where(lane == slot + 32 * e, table, 0.0), axis=1, keepdims=True))
@@ -297,7 +302,7 @@
     far = slots.shape[0]
     count, width = everyone.shape
     tokens = count // (far * near)
-    pair = 2
+    pair = 4
     return pl.pallas_call(
         functools.partial(owner_kernel, capacity, near, tokens, pair),
         grid=(far // pair,),
@@ -318,7 +323,7 @@
     near = NEAR
     far = sources // near
     order = row_order(sources)
-    near_groups = [[f * near + n for n in range(near)] for f in range(far)]
+    near_groups = [[f * near + near_member(q) for q in range(near)] for f in range(far)]
     turn = far // 2
     far_groups = [[(f + turn) % far * near + n for f in range(far)] for n in range(near)]
     experts = local * sources

time: 217 us -> 216 us (level)
  the two profiles are of different devices: /device:TPU:1 before, /device:TPU:25 now
where the time goes in v7:
time: 216 us; the launch traced here: 215 us
  waiting for transfers between devices  69.8 us (32%)
  starting transfers between devices  69.6 us (32%)
  blocking collectives  41.3 us (19%)
  Pallas kernels  17.9 us (8%)
  between operations  14.1 us (7%)
    all_to_all x2, waiting for transfers between devices, exchange(): lax.all_to_all(array, EXP, 0, 0, tiled=True, axis_index_groups=groups)  45.9 us
    all_to_all x2, starting transfers between devices, exchange(): lax.all_to_all(array, EXP, 0, 0, tiled=True, axis_index_groups=groups)  45.1 us
    all_to_all x2, blocking collectives, exchange(): lax.all_to_all(array, EXP, 0, 0, tiled=True, axis_index_groups=groups)  41.3 us
    ppermute x6, starting transfers between devices, ring_parts(): lax.ppermute(array, axis, [(i, (i + shift) % size) for i in range(size)])  18.1 us
    pallas_call x8, Pallas kernels, call(): pl.pallas_call(kernel, out_shape=[shaped(*out) for out in outs], in_specs...  14.4 us
    all_gather x1, waiting for transfers between devices, step(): everyone = lax.all_gather(cotangent, EXP, tiled=True)  12.2 us
    all_to_all x1, starting transfers between devices, step(): dots = lax.all_to_all(partial_dots, CTX, 0, 0, tiled=True)  6.41 us
    ppermute x6, waiting for transfers between devices, ring_parts(): lax.ppermute(array, axis, [(i, (i + shift) % size) for i in range(size)])  6.33 us
  transfers between devices with their start and end apart: 10, of which 7 were waited for; matrix products, arithmetic and copies ran while one was open for 1% of the time, Pallas kernels for 7%

profile of v7, /device:TPU:25, one launch (start us, length us, event | category | flops | bytes accessed | tf_op | source)
XLA Modules:
  0.0 215.3 jit_solution(5405220290543713640)
XLA Ops:
  7.2 2.5 %shard_map.93 = bf16[64,24,256]{2,1,0:T(8,128)(2,1)} custom-call(bf16[192,192]{1,0:T(8,128)(2,1)} %constant.2.clone.perm_ref, bf16[2,768,256]{2,1,0:T(8,128)(2,1)} %in_ref.1), custom_call_target="tpu_custom_call" | custom-call | tf_op jit(solution)/shard_map/pallas_call | solution.py:74
  9.6 34.9 %all-to-all-start = ((bf16[64,24,256]{2,1,0:T(8,128)(2,1)}), bf16[64,24,256]{2,1,0:T(8,128)(2,1)S(1)}, u32[]{:S(2)}, u32[]{:S(2)}) async-start(bf16[64,24,256]{2,1,0:T(8,128)(2,1)} %shard_map.93), calls=%async_computation | async-start | bytes 1572864 | tf_op jit(solution)/shard_map/all_to_all | solution.py:37
  44.6 0.0 all-gather.2.cloned.1.call-start
  44.6 0.7 all-gather.2.cloned.1.call-update
  45.3 1.2 fusion
  46.5 4.4 %collective-permute-start.2 = (f32[128,128]{1,0:T(8,128)S(1)}, f32[128,128]{1,0:T(8,128)S(1)}, u32[]{:S(2)}, u32[]{:S(2)}) collective-permute-start(f32[128,128]{1,0:T(8,128)S(1)} %fusion), channel_id=1, source_target_pairs={{0,192},{64,0},{128,64},{192,128},{1,193},{65,1},{129,65},{193,129... | collective-permute-start | bytes 196616 | tf_op jit(solution)/shard_map/ppermute | solution.py:44
  50.9 2.4 %collective-permute-start.1 = (f32[128,128]{1,0:T(8,128)S(1)}, f32[128,128]{1,0:T(8,128)S(1)}, u32[]{:S(2)}, u32[]{:S(2)}) collective-permute-start(f32[128,128]{1,0:T(8,128)S(1)} %fusion), channel_id=1, source_target_pairs={{0,128},{64,192},{128,0},{192,64},{1,129},{65,193},{129,1},{193,65... | collective-permute-start | bytes 196616 | tf_op jit(solution)/shard_map/ppermute | solution.py:44
  53.3 2.5 %collective-permute-start = (f32[128,128]{1,0:T(8,128)S(1)}, f32[128,128]{1,0:T(8,128)S(1)}, u32[]{:S(2)}, u32[]{:S(2)}) collective-permute-start(f32[128,128]{1,0:T(8,128)S(1)} %fusion), channel_id=1, source_target_pairs={{0,64},{64,128},{128,192},{192,0},{1,65},{65,129},{129,193},{193,1... | collective-permute-start | bytes 196616 | tf_op jit(solution)/shard_map/ppermute | solution.py:44
  55.9 1.8 collective-permute-done.1
  57.7 2.1 collective-permute-done
  59.9 2.4 %collective-permute-start.5 = (f32[128,128]{1,0:T(8,128)S(1)}, f32[128,128]{1,0:T(8,128)S(1)}, u32[]{:S(2)}, u32[]{:S(2)}) collective-permute-start(f32[128,128]{1,0:T(8,128)S(1)} %add_add_fusion.1), channel_id=1, source_target_pairs={{0,768},{256,0},{512,256},{768,512},{1,769},{257,1},{513,257},{769... | collective-permute-start | bytes 196616 | tf_op jit(solution)/shard_map/ppermute | solution.py:44
  62.2 2.6 %collective-permute-start.4 = (f32[128,128]{1,0:T(8,128)S(1)}, f32[128,128]{1,0:T(8,128)S(1)}, u32[]{:S(2)}, u32[]{:S(2)}) collective-permute-start(f32[128,128]{1,0:T(8,128)S(1)} %add_add_fusion.1), channel_id=1, source_target_pairs={{0,512},{256,768},{512,0},{768,256},{1,513},{257,769},{513,1},{769... | collective-permute-start | bytes 196616 | tf_op jit(solution)/shard_map/ppermute | solution.py:44
  64.8 3.8 %collective-permute-start.3 = (f32[128,128]{1,0:T(8,128)S(1)}, f32[128,128]{1,0:T(8,128)S(1)}, u32[]{:S(2)}, u32[]{:S(2)}) collective-permute-start(f32[128,128]{1,0:T(8,128)S(1)} %add_add_fusion.1), channel_id=1, source_target_pairs={{0,256},{256,512},{512,768},{768,0},{1,257},{257,513},{513,769},{7... | collective-permute-start | bytes 196616 | tf_op jit(solution)/shard_map/ppermute | solution.py:44
  68.6 0.4 collective-permute-done.4
  69.0 1.9 collective-permute-done.3
  71.0 0.6 add_add_fusion.logits_ref
  71.6 3.7 %shard_map.94 = (f32[128,128]{1,0:T(8,128)S(1)}, f32[24,128]{1,0:T(8,128)S(1)}, f32[8,128]{1,0:T(8,128)S(1)}, bf16[3,128,1536]{2,1,0:T(8,128)(2,1)}, f32[8,8,128]{2,1,0:T(8,128)S(1)}) custom-call(f32[128,128]{1,0:T(8,128)} %add_add_fusion.logits_ref, s32[8,128]{1,0:T(8,128)} %bitcast.7), custom_call_target="tpu_custom_call" | custom-call | tf_op jit(solution)/shard_map/pallas_call | solution.py:74
  75.4 45.9 %all-to-all-done.rows_ref = bf16[64,24,256]{2,1,0:T(8,128)(2,1)S(1)} async-done(((bf16[64,24,256]{2,1,0:T(8,128)(2,1)}), bf16[64,24,256]{2,1,0:T(8,128)(2,1)S(1)}, u32[]{:S(2)}, u32[]{:S(2)}) %all-to-all-start) | async-done | bytes 786464 | tf_op jit(solution)/shard_map/all_to_all | solution.py:37
  121.2 2.3 %shard_map.96 = f32[16,8,128]{2,1,0:T(8,128)} custom-call(bf16[64,24,256]{2,1,0:T(8,128)(2,1)S(1)} %all-to-all-done.rows_ref, bf16[128,256]{1,0:T(8,128)(2,1)} %cot_ref.1, f32[8,128]{1,0:T(8,128)S(1)} %get-tuple-element.12.row_ref), custom_call_target="tpu_custom_call" | custom-call | tf_op jit(solution)/shard_map/pallas_call | solution.py:74
  123.5 6.4 %all-to-all-start.1 = ((f32[16,8,128]{2,1,0:T(8,128)}), f32[16,8,128]{2,1,0:T(8,128)S(1)}, u32[]{:S(2)}, u32[]{:S(2)}) async-start(f32[16,8,128]{2,1,0:T(8,128)} %shard_map.96), calls=%async_computation.1 | async-start | bytes 131072 | tf_op jit(solution)/shard_map/all_to_all | solution.py:363
  129.9 0.1 copy.10
  130.0 4.7 %all-to-all-done.1.parts_ref = f32[16,8,128]{2,1,0:T(8,128)S(1)} async-done(((f32[16,8,128]{2,1,0:T(8,128)}), f32[16,8,128]{2,1,0:T(8,128)S(1)}, u32[]{:S(2)}, u32[]{:S(2)}) %all-to-all-start.1) | async-done | bytes 65568 | tf_op jit(solution)/shard_map/all_to_all | solution.py:363
  134.7 1.0 shard_map.97
  135.7 8.5 %all_to_all.25.in_ref = f32[8,40,128]{2,1,0:T(8,128)S(1)} all-to-all(f32[8,40,128]{2,1,0:T(8,128)S(1)} %get-tuple-element.17), channel_id=1, replica_groups={{5,6,7,0,1,2,3,4},{13,14,15,8,9,10,11,12},{21,22,23,16,17,18,19,20},{29..., dimensions={0} | all-to-all | bytes 327680 | tf_op jit(solution)/shard_map/all_to_all | solution.py:37
  144.2 32.8 %all_to_all.26.in_ref.slots_ref = f32[8,40,128]{2,1,0:T(8,128)S(1)} all-to-all(f32[8,40,128]{2,1,0:T(8,128)S(1)} %shard_map.99), channel_id=1, replica_groups={{32,40,48,56,0,8,16,24},{33,41,49,57,1,9,17,25},{34,42,50,58,2,10,18,26..., dimensions={0} | all-to-all | bytes 327680 | tf_op jit(solution)/shard_map/all_to_all | solution.py:37
  177.0 0.7 shard_map.100
  177.7 10.2 %all-to-all-start.4 = ((f32[8,32,128]{2,1,0:T(8,128)}), f32[8,32,128]{2,1,0:T(8,128)S(1)}, u32[]{:S(2)}, u32[]{:S(2)}) async-start(f32[8,32,128]{2,1,0:T(8,128)} %shard_map.100), calls=%async_computation.4 | async-start | bytes 262144 | tf_op jit(solution)/shard_map/all_to_all | solution.py:37
  187.9 2.4 %shard_map.95 = bf16[128,256]{1,0:T(8,128)(2,1)} custom-call(bf16[64,24,256]{2,1,0:T(8,128)(2,1)S(1)} %all-to-all-done.rows_ref, bf16[3,128,1536]{2,1,0:T(8,128)(2,1)} %get-tuple-element.11.wt_ref), custom_call_target="tpu_custom_call" | custom-call | tf_op jit(solution)/shard_map/pallas_call | solution.py:74
  190.2 1.9 shard_map.98
  192.1 12.2 %all-gather.2.cloned.1.call-done.all_ref = bf16[8192,256]{1,0:T(8,128)(2,1)} async-done(((bf16[128,256]{1,0:T(8,128)(2,1)}), bf16[8192,256]{1,0:T(8,128)(2,1)}) %all-gather.2.cloned.1.call-update) | async-done | bytes 4194320 | tf_op jit(solution)/shard_map/all_gather | solution.py:335
  204.3 3.5 %shard_map.101 = bf16[2,768,256]{2,1,0:T(8,128)(2,1)} custom-call(f32[8,40,128]{2,1,0:T(8,128)S(1)} %all_to_all.26.in_ref.slots_ref, bf16[8192,256]{1,0:T(8,128)(2,1)} %all-gather.2.cloned.1.call-done.all_ref), custom_call_target="tpu_custom_call" | custom-call | tf_op jit(solution)/shard_map/pallas_call | solution.py:306
  207.8 0.7 copy.12
  (7 shorter events, 0.1 us)
Async XLA Ops:
  7.2 122.8 %copy-start = (bf16[128,256]{1,0:T(8,128)(2,1)S(1)}, bf16[128,256]{1,0:T(8,128)(2,1)}, u32[]{:S(2)}) copy-start(bf16[128,256]{1,0:T(8,128)(2,1)} %param.6) | copy-start | bytes 196612
  9.6 111.6 %all-to-all-start = ((bf16[64,24,256]{2,1,0:T(8,128)(2,1)}), bf16[64,24,256]{2,1,0:T(8,128)(2,1)S(1)}, u32[]{:S(2)}, u32[]{:S(2)}) async-start(bf16[64,24,256]{2,1,0:T(8,128)(2,1)} %shard_map.93), calls=%async_computation | async-start | bytes 1572864 | tf_op jit(solution)/shard_map/all_to_all | solution.py:37
  44.6 159.8 %all-gather.2.cloned.1.call-start = ((), (), s32[]{:S(2)}) async-start(), calls=%async_computation.5 | async-start | bytes 4259840 | tf_op jit(solution)/shard_map/all_gather | solution.py:335
  46.5 9.4 %collective-permute-start.2 = (f32[128,128]{1,0:T(8,128)S(1)}, f32[128,128]{1,0:T(8,128)S(1)}, u32[]{:S(2)}, u32[]{:S(2)}) collective-permute-start(f32[128,128]{1,0:T(8,128)S(1)} %fusion), channel_id=1, source_target_pairs={{0,192},{64,0},{128,64},{192,128},{1,193},{65,1},{129,65},{193,129... | collective-permute-start | bytes 196616 | tf_op jit(solution)/shard_map/ppermute | solution.py:44
  50.9 6.8 %collective-permute-start.1 = (f32[128,128]{1,0:T(8,128)S(1)}, f32[128,128]{1,0:T(8,128)S(1)}, u32[]{:S(2)}, u32[]{:S(2)}) collective-permute-start(f32[128,128]{1,0:T(8,128)S(1)} %fusion), channel_id=1, source_target_pairs={{0,128},{64,192},{128,0},{192,64},{1,129},{65,193},{129,1},{193,65... | collective-permute-start | bytes 196616 | tf_op jit(solution)/shard_map/ppermute | solution.py:44
  53.3 6.5 %collective-permute-start = (f32[128,128]{1,0:T(8,128)S(1)}, f32[128,128]{1,0:T(8,128)S(1)}, u32[]{:S(2)}, u32[]{:S(2)}) collective-permute-start(f32[128,128]{1,0:T(8,128)S(1)} %fusion), channel_id=1, source_target_pairs={{0,64},{64,128},{128,192},{192,0},{1,65},{65,129},{129,193},{193,1... | collective-permute-start | bytes 196616 | tf_op jit(solution)/shard_map/ppermute | solution.py:44
  59.9 8.8 %collective-permute-start.5 = (f32[128,128]{1,0:T(8,128)S(1)}, f32[128,128]{1,0:T(8,128)S(1)}, u32[]{:S(2)}, u32[]{:S(2)}) collective-permute-start(f32[128,128]{1,0:T(8,128)S(1)} %add_add_fusion.1), channel_id=1, source_target_pairs={{0,768},{256,0},{512,256},{768,512},{1,769},{257,1},{513,257},{769... | collective-permute-start | bytes 196616 | tf_op jit(solution)/shard_map/ppermute | solution.py:44
  62.2 6.8 %collective-permute-start.4 = (f32[128,128]{1,0:T(8,128)S(1)}, f32[128,128]{1,0:T(8,128)S(1)}, u32[]{:S(2)}, u32[]{:S(2)}) collective-permute-start(f32[128,128]{1,0:T(8,128)S(1)} %add_add_fusion.1), channel_id=1, source_target_pairs={{0,512},{256,768},{512,0},{768,256},{1,513},{257,769},{513,1},{769... | collective-permute-start | bytes 196616 | tf_op jit(solution)/shard_map/ppermute | solution.py:44
  64.8 6.2 %collective-permute-start.3 = (f32[128,128]{1,0:T(8,128)S(1)}, f32[128,128]{1,0:T(8,128)S(1)}, u32[]{:S(2)}, u32[]{:S(2)}) collective-permute-start(f32[128,128]{1,0:T(8,128)S(1)} %add_add_fusion.1), channel_id=1, source_target_pairs={{0,256},{256,512},{512,768},{768,0},{1,257},{257,513},{513,769},{7... | collective-permute-start | bytes 196616 | tf_op jit(solution)/shard_map/ppermute | solution.py:44
  123.5 11.2 %all-to-all-start.1 = ((f32[16,8,128]{2,1,0:T(8,128)}), f32[16,8,128]{2,1,0:T(8,128)S(1)}, u32[]{:S(2)}, u32[]{:S(2)}) async-start(f32[16,8,128]{2,1,0:T(8,128)} %shard_map.96), calls=%async_computation.1 | async-start | bytes 131072 | tf_op jit(solution)/shard_map/all_to_all | solution.py:363
  177.7 30.1 %all-to-all-start.4 = ((f32[8,32,128]{2,1,0:T(8,128)}), f32[8,32,128]{2,1,0:T(8,128)S(1)}, u32[]{:S(2)}, u32[]{:S(2)}) async-start(f32[8,32,128]{2,1,0:T(8,128)} %shard_map.100), calls=%async_computation.4 | async-start | bytes 262144 | tf_op jit(solution)/shard_map/all_to_all | solution.py:37
Sparse Core Ops, SparseCore 0:
  48.1 156.2 all-gather.1
